TPU v7x, 32 devices: a whole 2x2x4 slice. The times are simulated.
32 devices in a mesh: win: 2 (over y), bl: 4 (over x, core), freq: 4 (over z).
Axes of the slice: x: 2, y: 2, z: 4, core: 2. Of those that a mesh axis runs over, the one named last changes fastest.
Arguments:
- vis: bfloat16 [64, 1536, 2, 512], P('bl', 'freq', None, 'win'), parts along dimension 3, may hold values from -6 to 6
- flags: int32 [64, 1536], P('bl', 'freq'), may hold values 0 or 1
- band: int32 [64], P('bl'), may hold values from 0 to 7
- group_id: int32 [64], P('bl'), may hold values from 0 to 7, as said below
Outputs:
- averaged: bfloat16 [8, 2, 512, 1536], P('bl', None, ('win', 'freq')), parts along dimension 2
There are 2 independent parts, one for each index of `win`. A program takes and returns all parts, laid end to end along the dimension named above; an argument that names none is the same for every part. Nothing has to cross between parts.
Inputs may be any that keep to these rules, and one draw needn't show every extreme that they name: `group_id`: of each aligned block of 16 baselines (those of one index of bl), at most 8 belong to the groups of one owner; in every draw one owner receives exactly 8 from every block.
All inputs are finite; a program needn't handle non-finite values. No bound on the sum of `flags` on one device may be relied on, other than what follows from the above.
Results may differ from a plain program's by a relative error of at most 0.0071.
Values may be sent and summed in bfloat16 or wider, within the bound.
A program may use at most 64 MiB of HBM per device.

v0:
```python
import math

import jax
import jax.numpy as jnp
from jax import lax
from jax.sharding import PartitionSpec as P

CH = 1536
DELAYS = 128
NBAND = 8
GPO = 2
CAP = 8


def fourier_tables(length):
    sample_index = jnp.arange(length, dtype=jnp.int32)
    phase_index = sample_index[:, None] * sample_index[None, :] % length
    angles = phase_index.astype(jnp.float32) * (2.0 * math.pi / length)
    cosine = jnp.cos(angles)
    sine_table = jnp.sin(angles)
    forward = jnp.concatenate(
        [jnp.concatenate([cosine, -sine_table], 1), jnp.concatenate([sine_table, cosine], 1)], 0
    )
    inverse = jnp.concatenate(
        [jnp.concatenate([cosine, sine_table], 1), jnp.concatenate([-sine_table, cosine], 1)], 0
    )
    return (forward.astype(jnp.bfloat16), inverse.astype(jnp.bfloat16))


def band_response(band, length, band_count):
    mode_index = jnp.arange(length, dtype=jnp.int32)
    signed_modes = (mode_index - length * (mode_index >= length // 2).astype(jnp.int32)).astype(
        jnp.float32
    )
    center = (band.astype(jnp.float32) - (band_count - 1) / 2.0) * (length / (4.0 * band_count))
    band_width = length / 32.0
    offset_ratio = (signed_modes[None, :] - center[:, None]) / band_width
    single = (0.15 + 0.85 / (1.0 + offset_ratio**4)) / length
    return jnp.concatenate([single, single], 1)


def make_basis(channels, modes):
    channel_index = jnp.arange(channels, dtype=jnp.int32)
    order_index = jnp.arange(modes, dtype=jnp.int32)
    phase_index = order_index[None, :] * (2 * channel_index[:, None] + 1) % (4 * channels)
    return jnp.cos(phase_index.astype(jnp.float32) * (math.pi / (2 * channels))).astype(
        jnp.bfloat16
    )


def per_device(vis, flags, band, group_id):
    base_count = vis.shape[0]
    chan_local = vis.shape[1]
    length = vis.shape[3]
    forward, inverse = fourier_tables(length)
    response = band_response(band, length, NBAND)
    flat_rows = vis.reshape(base_count * chan_local, 2 * length)
    spectra = jnp.dot(flat_rows, forward, preferred_element_type=jnp.float32).reshape(
        base_count, chan_local, 2 * length
    )
    spectra = (spectra * response[:, None, :]).astype(jnp.bfloat16)
    fringe = jnp.dot(
        spectra.reshape(base_count * chan_local, 2 * length),
        inverse,
        preferred_element_type=jnp.float32,
    )
    fringe = fringe.astype(jnp.bfloat16).reshape(base_count, chan_local, 2, length)
    shards = lax.axis_size("freq")
    time_local = length // shards
    weight_local = (1.0 - flags.astype(jnp.float32)).astype(jnp.bfloat16)
    weight_tiled = jnp.broadcast_to(
        weight_local[:, :, None, None], (base_count, chan_local, 1, shards)
    )
    delay_basis = make_basis(CH, DELAYS)
    basis_wide = delay_basis.astype(jnp.float32)
    ridge = CH / 64.0 * jnp.eye(DELAYS, dtype=jnp.float32)

    def one_normal(weight_row):
        weighted_basis = weight_row[:, None] * delay_basis
        return jnp.dot(weighted_basis.T, delay_basis, preferred_element_type=jnp.float32) + ridge

    received = lax.all_to_all(fringe, "freq", split_axis=3, concat_axis=1, tiled=True)
    weight_items = lax.all_to_all(weight_tiled, "freq", split_axis=3, concat_axis=1, tiled=True)
    item_count = received.shape[0]
    weight_half = weight_items.reshape(item_count, CH)
    weight_full = weight_half.astype(jnp.float32)
    normal = lax.map(one_normal, weight_half, batch_size=8)
    factor = jnp.linalg.cholesky(normal)
    masked = received * weight_half[:, :, None, None]
    projected = jnp.einsum("bcrt,ck->bkrt", masked, delay_basis, preferred_element_type=jnp.float32)
    projected = projected.reshape(item_count, DELAYS, 2 * time_local)
    half_solved = lax.linalg.triangular_solve(factor, projected, left_side=True, lower=True)
    coefficients = lax.linalg.triangular_solve(
        factor, half_solved, left_side=True, lower=True, transpose_a=True
    )
    coefficients = coefficients.reshape(item_count, DELAYS, 2, time_local)
    fitted = jnp.einsum("bkrt,ck->brtc", coefficients, basis_wide, precision=lax.Precision.HIGHEST)
    reordered = jnp.transpose(received, (0, 2, 3, 1)).astype(jnp.float32)
    cleaned = (weight_full[:, None, None, :] * (reordered - fitted)).astype(jnp.bfloat16)
    row_width = 2 * time_local * CH
    cleaned_rows = cleaned.reshape(base_count, row_width)
    owners = lax.axis_size("bl")
    owner_of = group_id // GPO
    owner_hits = (owner_of[:, None] == jnp.arange(owners, dtype=jnp.int32)[None, :]).astype(
        jnp.int32
    )
    before_me = jnp.cumsum(owner_hits, axis=0) - owner_hits
    slot_of = jnp.sum(before_me * owner_hits, 1)
    target = owner_of * CAP + slot_of
    outgoing = jnp.zeros((owners * CAP, row_width), jnp.bfloat16).at[target].set(cleaned_rows)
    outgoing_ids = jnp.full((owners * CAP,), -1, jnp.int32).at[target].set(group_id)
    arrived, arrived_ids = (
        lax.all_to_all(
            outgoing.reshape(owners, CAP, row_width), "bl", split_axis=0, concat_axis=0, tiled=True
        ),
        lax.all_to_all(
            outgoing_ids.reshape(owners, CAP), "bl", split_axis=0, concat_axis=0, tiled=True
        ),
    )
    local_ids = arrived_ids.reshape(owners * CAP) - lax.axis_index("bl") * GPO
    select = (local_ids[None, :] == jnp.arange(GPO, dtype=jnp.int32)[:, None]).astype(jnp.bfloat16)
    group_sums = jnp.dot(
        select, arrived.reshape(owners * CAP, row_width), preferred_element_type=jnp.float32
    )
    counts = jnp.sum(select.astype(jnp.float32), 1)
    averaged = (group_sums / jnp.maximum(counts, 1.0)[:, None]).astype(jnp.bfloat16)
    return averaged.reshape(GPO, 2, time_local, CH)


def solution(mesh):
    in_specs = (P("bl", "freq", None, "win"), P("bl", "freq"), P("bl"), P("bl"))
    out_specs = P("bl", None, ("win", "freq"), None)
    return jax.shard_map(
        per_device, mesh=mesh, in_specs=in_specs, out_specs=out_specs, check_vma=False
    )
```

profile of v0, /device:TPU:0, one launch (start us, length us, event | category | flops | bytes accessed | tf_op | source)
XLA Modules:
  0.0 998.1 jit_solution(16450803121704375823)
XLA Ops:
  1.4 6.3 all-to-all-start.1
  11.4 5.4 mul.224
  16.7 15.1 %copy.65 = f32[64,8,16,384]{3,1,2,0:T(8,128)} copy(f32[64,8,16,384]{3,2,1,0:T(8,128)} %bitcast.103) | data formatting | bytes 25165824
  35.6 15.2 %convolution_convert_fusion = bf16[6144,512]{1,0:T(8,128)(2,1)} fusion(f32[6144,512]{0,1:T(8,128)} %bitcast.107, bf16[6144,512]{1,0:T(8,128)(2,1)} %bitcast.112, bf16[256,256]{1,0:T(8,128)(2,1)S(1)} %get-tuple-element.87, bf16[256,256]{1,0:T(8,128)(2,1)} %fusion.71, bf16[256,256]{1,0:T(8,128)(2,1)S(1)} %get-tuple-element.86), kind=kOutput, calls=%fused_computation.37 | convolution fusion | flops 6456082432 | bytes 25559040 | tf_op jit(solution)/shard_map/dot_general | solution.py:62
  50.7 9.8 reshape.96
  60.5 21.3 %copy.46 = bf16[16,384,2,256]{1,2,0,3:T(2,128)(2,1)} copy(bf16[16,384,2,256]{3,2,1,0:T(2,128)(2,1)} %reshape.96) | data formatting | bytes 12582912 | tf_op jit(solution)/shard_map/reshape | solution.py:67
  81.8 5.4 all-to-all-start.2
  88.9 15.2 %while.14 = (s32[]{:T(128)}, f32[2,8,128,128]{3,2,1,0:T(8,128)S(1)}, bf16[2,8,1536]{2,1,0:T(8,128)(2,1)S(1)}, s32[1536]{0:T(1024)S(1)}, s32[]{:T(128)}) while((s32[]{:T(128)}, f32[2,8,128,128]{3,2,1,0:T(8,128)S(1)}, bf16[2,8,1536]{2,1,0:T(8,128)(2,1)S(1)}, s32[1536]{0:T(1024)S(1)}, s32[]{:T(128)}) %tuple.36), condition=%wide.region_4.5_spmd.clone.clone, body=%wide.region_3.4_spmd.clone.clone.sunk | while | flops 408322048 | bytes 2316357 | solution.py:87
  105.6 188.3 %custom-call.9 = f32[16,128,128]{2,1,0:T(8,128)S(1)} custom-call(f32[16,128,128]{2,1,0:T(8,128)} %fusion.36), custom_call_target="Cholesky" | custom-call | tf_op jit(solution)/shard_map/jit(cholesky)/cholesky | solution.py:88
  294.3 157.2 %custom-call.10 = f32[16,1,128,128]{2,3,1,0:T(8,128)S(1)} custom-call(f32[16,1,128,128]{3,2,1,0:T(8,128)S(1)} %select_bitcast_fusion), custom_call_target="InvertDiagBlocksLowerTriangular" | custom-call | tf_op jit(solution)/shard_map/triangular_solve | solution.py:93
  468.8 9.8 fusion.34
  478.6 6.1 copy.66
  489.7 356.2 %while.13 = (s32[]{:T(128)}, bf16[32,196608]{1,0:T(8,128)(2,1)}, s32[16]{0:T(128)S(1)}, bf16[16,196608]{1,0:T(8,128)(2,1)}, s32[]{:T(128)}, /*index=5*/s32[2]{0:T(128)S(1)}, s32[1]{0:T(128)}, s32[]{:T(128)}) while((s32[]{:T(128)}, bf16[32,196608]{1,0:T(8,128)(2,1)}, s32[16]{0:T(128)S(1)}, bf16[16,196608]{1,0:T(8,128)(2,1)}, s32[]{:T(128)}, ...), condition=%wide.while_cond, body=%wide.while_body.sunk | while | flops 196619 | bytes 1966207 | solution.py:110
  496.4 15.5 %dynamic-update-slice.6 = bf16[32,196608]{1,0:T(8,128)(2,1)} dynamic-update-slice(bf16[32,196608]{1,0:T(8,128)(2,1)} %get-tuple-element.162, bf16[1,196608]{1,0:T(2,128)(2,1)S(1)} %broadcast_select_fusion.2, s32[]{:T(128)} %bitcast.95, s32[]{:T(128)} %constant.123.clone.1..sunk) | dynamic-update-slice | bytes 786436 | tf_op jit(solution)/shard_map/scatter
  518.7 15.6 %dynamic-update-slice.6 = bf16[32,196608]{1,0:T(8,128)(2,1)} dynamic-update-slice(bf16[32,196608]{1,0:T(8,128)(2,1)} %get-tuple-element.162, bf16[1,196608]{1,0:T(2,128)(2,1)S(1)} %broadcast_select_fusion.2, s32[]{:T(128)} %bitcast.95, s32[]{:T(128)} %constant.123.clone.1..sunk) | dynamic-update-slice | bytes 786436 | tf_op jit(solution)/shard_map/scatter
  541.0 15.5 %dynamic-update-slice.6 = bf16[32,196608]{1,0:T(8,128)(2,1)} dynamic-update-slice(bf16[32,196608]{1,0:T(8,128)(2,1)} %get-tuple-element.162, bf16[1,196608]{1,0:T(2,128)(2,1)S(1)} %broadcast_select_fusion.2, s32[]{:T(128)} %bitcast.95, s32[]{:T(128)} %constant.123.clone.1..sunk) | dynamic-update-slice | bytes 786436 | tf_op jit(solution)/shard_map/scatter
  563.2 15.5 %dynamic-update-slice.6 = bf16[32,196608]{1,0:T(8,128)(2,1)} dynamic-update-slice(bf16[32,196608]{1,0:T(8,128)(2,1)} %get-tuple-element.162, bf16[1,196608]{1,0:T(2,128)(2,1)S(1)} %broadcast_select_fusion.2, s32[]{:T(128)} %bitcast.95, s32[]{:T(128)} %constant.123.clone.1..sunk) | dynamic-update-slice | bytes 786436 | tf_op jit(solution)/shard_map/scatter
  585.5 15.5 %dynamic-update-slice.6 = bf16[32,196608]{1,0:T(8,128)(2,1)} dynamic-update-slice(bf16[32,196608]{1,0:T(8,128)(2,1)} %get-tuple-element.162, bf16[1,196608]{1,0:T(2,128)(2,1)S(1)} %broadcast_select_fusion.2, s32[]{:T(128)} %bitcast.95, s32[]{:T(128)} %constant.123.clone.1..sunk) | dynamic-update-slice | bytes 786436 | tf_op jit(solution)/shard_map/scatter
  607.7 15.5 %dynamic-update-slice.6 = bf16[32,196608]{1,0:T(8,128)(2,1)} dynamic-update-slice(bf16[32,196608]{1,0:T(8,128)(2,1)} %get-tuple-element.162, bf16[1,196608]{1,0:T(2,128)(2,1)S(1)} %broadcast_select_fusion.2, s32[]{:T(128)} %bitcast.95, s32[]{:T(128)} %constant.123.clone.1..sunk) | dynamic-update-slice | bytes 786436 | tf_op jit(solution)/shard_map/scatter
  630.0 15.6 %dynamic-update-slice.6 = bf16[32,196608]{1,0:T(8,128)(2,1)} dynamic-update-slice(bf16[32,196608]{1,0:T(8,128)(2,1)} %get-tuple-element.162, bf16[1,196608]{1,0:T(2,128)(2,1)S(1)} %broadcast_select_fusion.2, s32[]{:T(128)} %bitcast.95, s32[]{:T(128)} %constant.123.clone.1..sunk) | dynamic-update-slice | bytes 786436 | tf_op jit(solution)/shard_map/scatter
  652.2 15.6 %dynamic-update-slice.6 = bf16[32,196608]{1,0:T(8,128)(2,1)} dynamic-update-slice(bf16[32,196608]{1,0:T(8,128)(2,1)} %get-tuple-element.162, bf16[1,196608]{1,0:T(2,128)(2,1)S(1)} %broadcast_select_fusion.2, s32[]{:T(128)} %bitcast.95, s32[]{:T(128)} %constant.123.clone.1..sunk) | dynamic-update-slice | bytes 786436 | tf_op jit(solution)/shard_map/scatter
  674.5 15.5 %dynamic-update-slice.6 = bf16[32,196608]{1,0:T(8,128)(2,1)} dynamic-update-slice(bf16[32,196608]{1,0:T(8,128)(2,1)} %get-tuple-element.162, bf16[1,196608]{1,0:T(2,128)(2,1)S(1)} %broadcast_select_fusion.2, s32[]{:T(128)} %bitcast.95, s32[]{:T(128)} %constant.123.clone.1..sunk) | dynamic-update-slice | bytes 786436 | tf_op jit(solution)/shard_map/scatter
  696.8 15.5 %dynamic-update-slice.6 = bf16[32,196608]{1,0:T(8,128)(2,1)} dynamic-update-slice(bf16[32,196608]{1,0:T(8,128)(2,1)} %get-tuple-element.162, bf16[1,196608]{1,0:T(2,128)(2,1)S(1)} %broadcast_select_fusion.2, s32[]{:T(128)} %bitcast.95, s32[]{:T(128)} %constant.123.clone.1..sunk) | dynamic-update-slice | bytes 786436 | tf_op jit(solution)/shard_map/scatter
  719.1 15.5 %dynamic-update-slice.6 = bf16[32,196608]{1,0:T(8,128)(2,1)} dynamic-update-slice(bf16[32,196608]{1,0:T(8,128)(2,1)} %get-tuple-element.162, bf16[1,196608]{1,0:T(2,128)(2,1)S(1)} %broadcast_select_fusion.2, s32[]{:T(128)} %bitcast.95, s32[]{:T(128)} %constant.123.clone.1..sunk) | dynamic-update-slice | bytes 786436 | tf_op jit(solution)/shard_map/scatter
  741.3 15.5 %dynamic-update-slice.6 = bf16[32,196608]{1,0:T(8,128)(2,1)} dynamic-update-slice(bf16[32,196608]{1,0:T(8,128)(2,1)} %get-tuple-element.162, bf16[1,196608]{1,0:T(2,128)(2,1)S(1)} %broadcast_select_fusion.2, s32[]{:T(128)} %bitcast.95, s32[]{:T(128)} %constant.123.clone.1..sunk) | dynamic-update-slice | bytes 786436 | tf_op jit(solution)/shard_map/scatter
  763.6 15.5 %dynamic-update-slice.6 = bf16[32,196608]{1,0:T(8,128)(2,1)} dynamic-update-slice(bf16[32,196608]{1,0:T(8,128)(2,1)} %get-tuple-element.162, bf16[1,196608]{1,0:T(2,128)(2,1)S(1)} %broadcast_select_fusion.2, s32[]{:T(128)} %bitcast.95, s32[]{:T(128)} %constant.123.clone.1..sunk) | dynamic-update-slice | bytes 786436 | tf_op jit(solution)/shard_map/scatter
  785.8 15.6 %dynamic-update-slice.6 = bf16[32,196608]{1,0:T(8,128)(2,1)} dynamic-update-slice(bf16[32,196608]{1,0:T(8,128)(2,1)} %get-tuple-element.162, bf16[1,196608]{1,0:T(2,128)(2,1)S(1)} %broadcast_select_fusion.2, s32[]{:T(128)} %bitcast.95, s32[]{:T(128)} %constant.123.clone.1..sunk) | dynamic-update-slice | bytes 786436 | tf_op jit(solution)/shard_map/scatter
  808.1 15.5 %dynamic-update-slice.6 = bf16[32,196608]{1,0:T(8,128)(2,1)} dynamic-update-slice(bf16[32,196608]{1,0:T(8,128)(2,1)} %get-tuple-element.162, bf16[1,196608]{1,0:T(2,128)(2,1)S(1)} %broadcast_select_fusion.2, s32[]{:T(128)} %bitcast.95, s32[]{:T(128)} %constant.123.clone.1..sunk) | dynamic-update-slice | bytes 786436 | tf_op jit(solution)/shard_map/scatter
  830.4 15.5 %dynamic-update-slice.6 = bf16[32,196608]{1,0:T(8,128)(2,1)} dynamic-update-slice(bf16[32,196608]{1,0:T(8,128)(2,1)} %get-tuple-element.162, bf16[1,196608]{1,0:T(2,128)(2,1)S(1)} %broadcast_select_fusion.2, s32[]{:T(128)} %bitcast.95, s32[]{:T(128)} %constant.123.clone.1..sunk) | dynamic-update-slice | bytes 786436 | tf_op jit(solution)/shard_map/scatter
  845.9 6.3 all-to-all-start.3
  852.5 137.9 %all-to-all-done.3 = bf16[4,8,196608]{2,1,0:T(8,128)(2,1)} async-done(((bf16[4,8,196608]{2,1,0:T(8,128)(2,1)}), bf16[4,8,196608]{2,1,0:T(8,128)(2,1)}, u32[]{:S(2)}, u32[]{:S(2)}) %all-to-all-start.3) | async-done | bytes 12582944 | tf_op jit(solution)/shard_map/all_to_all | solution.py:113
  990.4 6.3 fusion.31
  (113 shorter events, 158.3 us)
Async XLA Ops:
  1.4 80.4 %all-to-all-start.1 = ((bf16[16,384,1,4]{1,0,2,3:T(8,128)(2,1)}), bf16[16,384,1,4]{1,0,2,3:T(8,128)(2,1)S(1)}, u32[]{:S(2)}, u32[]{:S(2)}) async-start(bf16[16,384,1,4]{1,0,2,3:T(8,128)(2,1)} %broadcast_in_dim.22), calls=%async_computation.1 | async-start | bytes 98304 | tf_op jit(solution)/shard_map/all_to_all | solution.py:83
  11.3 20.5 %slice-start = ((s8[6291456]{0:T(1024)(128)(4,1)}), s8[4194304]{0:T(1024)(128)(4,1)S(1)}, s32[]{:S(2)}) async-start(s8[6291456]{0:T(1024)(128)(4,1)} %bitcast.109), calls=%async_computation.4 | async-start | bytes 8388608
  16.7 15.1 %slice-start.1 = ((s8[6291456]{0:T(1024)(128)(4,1)}), s8[2097152]{0:T(1024)(128)(4,1)S(1)}, s32[]{:S(2)}) async-start(s8[6291456]{0:T(1024)(128)(4,1)} %bitcast.109), calls=%async_computation.5 | async-start | bytes 4194304
  81.8 5.4 copy-start.1
  81.8 369.7 %all-to-all-start.2 = ((bf16[16,384,2,256]{1,2,0,3:T(2,128)(2,1)}), bf16[16,384,2,256]{1,2,0,3:T(2,128)(2,1)}, u32[]{:S(2)}, u32[]{:S(2)}) async-start(bf16[16,384,2,256]{1,2,0,3:T(2,128)(2,1)} %copy.46), calls=%async_computation.2 | async-start | bytes 12582912 | tf_op jit(solution)/shard_map/all_to_all | solution.py:82
  451.5 394.4 %all-to-all-start = ((s32[4,1,8]{2,1,0:T(1,128)}), s32[4,1,8]{2,1,0:T(1,128)S(1)}, u32[]{:S(2)}, u32[]{:S(2)}) async-start(s32[4,1,8]{2,1,0:T(1,128)} %bitcast), calls=%async_computation | async-start | bytes 4096 | tf_op jit(solution)/shard_map/all_to_all | solution.py:116
  484.7 5.0 copy-start
  845.9 144.5 %all-to-all-start.3 = ((bf16[4,8,196608]{2,1,0:T(8,128)(2,1)}), bf16[4,8,196608]{2,1,0:T(8,128)(2,1)}, u32[]{:S(2)}, u32[]{:S(2)}) async-start(bf16[4,8,196608]{2,1,0:T(8,128)(2,1)} %bitcast.102), calls=%async_computation.3 | async-start | bytes 25165824 | tf_op jit(solution)/shard_map/all_to_all | solution.py:113
where the time goes:
time: 1010 us; the launch traced here: 998 us
  other arithmetic  457 us (45%)
  local copies, waits for them, and re-layouts  334 us (33%)
  waiting for transfers between devices  138 us (14%)
  matrix products  46.4 us (5%)
  starting transfers between devices  21.5 us (2%)
    scatter x32, local copies, waits for them, and re-layouts  258 us
    another operation x4, other arithmetic, per_device(): factor = jnp.linalg.cholesky(normal)  189 us
    another operation x3, other arithmetic, per_device(): lax.linalg.triangular_solve(factor, half_solved, left_side=True, lower=Tr...  157 us
    all_to_all x1, waiting for transfers between devices, per_device(): lax.all_to_all(outgoing.reshape(owners, CAP, row_width), 'bl', split_axis...  138 us
    scatter x32, other arithmetic  98.1 us
    reshape x2, local copies, waits for them, and re-layouts, per_device(): fringe.astype(jnp.bfloat16).reshape(base_count, chan_local, 2, length)  31 us
    unnamed x13, local copies, waits for them, and re-layouts  25.9 us
  transfers between devices with their start and end apart: 4, of which 1 were waited for; matrix products, arithmetic and copies ran while one was open for 83% of the time, Pallas kernels for 0%

commit v1 on v0

v1 whole, which is shorter than its diff:
```python
import functools
import math

import jax
import jax.numpy as jnp
from jax import lax
from jax.experimental import pallas as pl
from jax.experimental.pallas import tpu as pltpu
from jax.sharding import PartitionSpec as P

CH = 1536
DELAYS = 128
NBAND = 8
GPO = 2
CAP = 8


def fourier_tables(length):
    sample_index = jnp.arange(length, dtype=jnp.int32)
    phase_index = sample_index[:, None] * sample_index[None, :] % length
    angles = phase_index.astype(jnp.float32) * (2.0 * math.pi / length)
    cosine = jnp.cos(angles)
    sine_table = jnp.sin(angles)
    forward = jnp.concatenate(
        [jnp.concatenate([cosine, -sine_table], 1), jnp.concatenate([sine_table, cosine], 1)], 0
    )
    return forward.astype(jnp.bfloat16)


def band_response(band, length, band_count):
    mode_index = jnp.arange(length, dtype=jnp.int32)
    signed_modes = (mode_index - length * (mode_index >= length // 2).astype(jnp.int32)).astype(
        jnp.float32
    )
    center = (band.astype(jnp.float32) - (band_count - 1) / 2.0) * (length / (4.0 * band_count))
    band_width = length / 32.0
    offset_ratio = (signed_modes[None, :] - center[:, None]) / band_width
    single = (0.15 + 0.85 / (1.0 + offset_ratio**4)) / length
    return jnp.concatenate([single, single], 1)


def make_basis(channels, modes):
    channel_index = jnp.arange(channels, dtype=jnp.int32)
    order_index = jnp.arange(modes, dtype=jnp.int32)
    phase_index = order_index[None, :] * (2 * channel_index[:, None] + 1) % (4 * channels)
    return jnp.cos(phase_index.astype(jnp.float32) * (math.pi / (2 * channels))).astype(
        jnp.bfloat16
    )


NT = (((1,), (1,)), ((), ()))
BIG = 48 * 1024 * 1024


def dot32(left, right):
    return jnp.dot(left, right, preferred_element_type=jnp.float32)


def halves(value):
    high = value.astype(jnp.bfloat16)
    return high, (value - high.astype(jnp.float32)).astype(jnp.bfloat16)


def dot_split(left, right):
    left_high, left_low = left
    right_high, right_low = right
    return dot32(left_high, right_high) + (
        dot32(left_high, right_low) + dot32(left_low, right_high)
    )


def filter_kernel(shards, re_ref, im_ref, fwd_ref, inv_ref, resp_ref, weight_ref, basis_ref,
                  fringe_ref, proj_ref):
    half = re_ref.shape[2]
    spectra = dot32(re_ref[0], fwd_ref[:half]) + dot32(im_ref[0], fwd_ref[half:])
    spectra = (spectra * resp_ref[0]).astype(jnp.bfloat16)
    fringe = lax.dot_general(inv_ref[...], spectra, NT, preferred_element_type=jnp.float32)
    fringe = (fringe * weight_ref[0]).astype(jnp.bfloat16)
    fringe_ref[0] = fringe
    projected = dot32(fringe, basis_ref[...])
    proj_ref[:, 0] = projected.reshape(shards, -1, projected.shape[1]).astype(jnp.bfloat16)


def inverse_kernel(batch, ridge, scales, start, weight_ref, basis_ref, basis_t_ref, out_ref):
    modes = out_ref.shape[1]
    eye = (
        lax.broadcasted_iota(jnp.int32, (modes, modes), 0)
        == lax.broadcasted_iota(jnp.int32, (modes, modes), 1)
    ).astype(jnp.float32)
    normals = [
        dot32(basis_t_ref[...] * weight_ref[i], basis_ref[...]) + ridge * eye for i in range(batch)
    ]
    first = scales[0]
    guess = [first * (2.0 * start * eye - start * start * normal) for normal in normals]
    normals = [halves(normal) for normal in normals]
    for scale in scales[1:]:
        guess_parts = [halves(value) for value in guess]
        product = [dot_split(n, g) for n, g in zip(normals, guess_parts)]
        change = [halves(2.0 * eye - value) for value in product]
        guess = [scale * dot_split(g, c) for g, c in zip(guess_parts, change)]
    for i in range(batch):
        out_ref[i] = guess[i]


def solve_kernel(batch, recv_ref, inverse_ref, out_ref):
    for i in range(batch):
        total = jnp.sum(recv_ref[:, i].astype(jnp.float32), axis=0)
        out_ref[i] = dot_split(halves(total), halves(inverse_ref[i])).astype(jnp.bfloat16)


def clean_kernel(ids_ref, fringe_ref, coef_ref, basis_t_ref, weight_ref, out_ref, total_ref):
    item = pl.program_id(0)

    @pl.when(item == 0)
    def _():
        total_ref[...] = jnp.zeros_like(total_ref)

    coef = coef_ref[:, 0].astype(jnp.float32)
    coef = coef.reshape(-1, coef.shape[2]).astype(jnp.bfloat16)
    fitted = dot32(coef, basis_t_ref[...]) * weight_ref[0]
    cleaned = fringe_ref[0].astype(jnp.float32) - fitted
    group = ids_ref[item]
    total_ref[group] += cleaned

    @pl.when(item == pl.num_programs(0) - 1)
    def _():
        out_ref[...] = total_ref[...].astype(jnp.bfloat16)


def newton_scales(low, high):
    scales = []
    value = (high + low) / (high - low)
    while True:
        doubled = 2.0 * value * value
        scales.append(doubled / (doubled - 1.0))
        value = doubled - 1.0
        if value > 1e6:
            return scales


def full(shape):
    return pl.BlockSpec(shape, lambda i, *rest: (0,) * len(shape))


def lead(shape):
    return pl.BlockSpec(shape, lambda i, *rest: (i,) + (0,) * (len(shape) - 1))


def second(shape):
    return pl.BlockSpec(shape, lambda i, *rest: (0, i) + (0,) * (len(shape) - 2))


def per_device(vis, flags, band, group_id):
    items, chan, _, length = vis.shape
    both = 2 * length
    shards = lax.axis_size("freq")
    owners = lax.axis_size("bl")
    groups = GPO * owners
    time_local = length // shards
    rows = 2 * time_local
    bf16, f32 = jnp.bfloat16, jnp.float32

    forward = fourier_tables(length)
    inverse_t = forward.reshape(2, shards, time_local, both)
    inverse_t = jnp.transpose(inverse_t, (1, 0, 2, 3)).reshape(both, both)
    response = band_response(band, length, NBAND).reshape(items, 1, both)
    basis = make_basis(CH, DELAYS)
    basis_t = basis.T
    basis_local = lax.dynamic_slice_in_dim(basis, lax.axis_index("freq") * chan, chan, 0)
    weight = 1.0 - flags.astype(f32)
    weight_rows = weight.reshape(items, 1, chan)
    weight_full = lax.all_gather(weight.astype(bf16), "freq", axis=1, tiled=True)
    weight_full = weight_full.reshape(items, 1, CH)

    fringe, projected = pl.pallas_call(
        functools.partial(filter_kernel, shards),
        grid=(items,),
        in_specs=[
            lead((1, chan, length)), lead((1, chan, length)), full((both, both)),
            full((both, both)), lead((1, 1, both)), lead((1, 1, chan)), full((chan, DELAYS)),
        ],
        out_specs=[lead((1, both, chan)), second((shards, 1, rows, DELAYS))],
        out_shape=[
            jax.ShapeDtypeStruct((items, both, chan), bf16),
            jax.ShapeDtypeStruct((shards, items, rows, DELAYS), bf16),
        ],
        compiler_params=pltpu.CompilerParams(vmem_limit_bytes=BIG),
        cost_estimate=pl.CostEstimate(
            flops=4 * items * chan * both * both, bytes_accessed=4 * items * chan * both,
            transcendentals=0,
        ),
    )(vis[:, :, 0, :], vis[:, :, 1, :], forward, inverse_t, response, weight_rows, basis_local)

    ridge = CH / 64.0
    high = ridge + 1.05 * CH
    batch = 4 if items % 4 == 0 else 1
    inverse = pl.pallas_call(
        functools.partial(
            inverse_kernel, batch, ridge, newton_scales(ridge, high), 2.0 / (ridge + high)
        ),
        grid=(items // batch,),
        in_specs=[lead((batch, 1, CH)), full((CH, DELAYS)), full((DELAYS, CH))],
        out_specs=lead((batch, DELAYS, DELAYS)),
        out_shape=jax.ShapeDtypeStruct((items, DELAYS, DELAYS), f32),
        compiler_params=pltpu.CompilerParams(vmem_limit_bytes=BIG),
        cost_estimate=pl.CostEstimate(
            flops=20_000_000_000, bytes_accessed=4 * items * DELAYS * DELAYS, transcendentals=0
        ),
    )(weight_full, basis, basis_t)

    received = lax.all_to_all(projected, "freq", split_axis=0, concat_axis=0, tiled=True)
    coefficients = pl.pallas_call(
        functools.partial(solve_kernel, batch),
        grid=(items // batch,),
        in_specs=[second((shards, batch, rows, DELAYS)), lead((batch, DELAYS, DELAYS))],
        out_specs=lead((batch, rows, DELAYS)),
        out_shape=jax.ShapeDtypeStruct((items, rows, DELAYS), bf16),
        compiler_params=pltpu.CompilerParams(vmem_limit_bytes=BIG),
    )(received, inverse)
    coefficients = lax.all_gather(coefficients, "freq")

    sums = pl.pallas_call(
        clean_kernel,
        grid_spec=pltpu.PrefetchScalarGridSpec(
            num_scalar_prefetch=1,
            grid=(items,),
            in_specs=[
                lead((1, both, chan)), second((shards, 1, rows, DELAYS)), full((DELAYS, chan)),
                lead((1, 1, chan)),
            ],
            out_specs=full((groups, both, chan)),
            scratch_shapes=[pltpu.VMEM((groups, both, chan), f32)],
        ),
        out_shape=jax.ShapeDtypeStruct((groups, both, chan), bf16),
        compiler_params=pltpu.CompilerParams(vmem_limit_bytes=BIG),
    )(group_id, fringe, coefficients, basis_local.T, weight_rows)

    arrived = lax.all_to_all(sums, "bl", split_axis=0, concat_axis=0, tiled=True)
    ids = lax.all_gather(group_id, "bl", tiled=True) - lax.axis_index("bl") * GPO
    hits = (ids[None, :] == jnp.arange(GPO, dtype=jnp.int32)[:, None]).astype(f32)
    counts = jnp.maximum(jnp.sum(hits, 1), 1.0)
    total = jnp.sum(arrived.reshape(owners, GPO, both, chan).astype(f32), 0)
    mean = (total / counts[:, None, None]).astype(bf16).reshape(GPO, shards, rows, chan)
    swapped = lax.all_to_all(
        jnp.transpose(mean, (1, 0, 2, 3)), "freq", split_axis=0, concat_axis=0, tiled=True
    )
    averaged = jnp.transpose(swapped, (1, 2, 0, 3))
    return averaged.reshape(GPO, 2, time_local, CH)


def solution(mesh):
    in_specs = (P("bl", "freq", None, "win"), P("bl", "freq"), P("bl"), P("bl"))
    out_specs = P("bl", None, ("win", "freq"), None)
    return jax.shard_map(
        per_device, mesh=mesh, in_specs=in_specs, out_specs=out_specs, check_vma=False
    )
```

time: 1010 us -> 263 us (0.26); the launches traced: 998 us -> 262 us
  other arithmetic: 457 us -> 9.15 us
  local copies, waits for them, and re-layouts: 334 us -> 29.6 us
  blocking collectives: 0 us -> 112 us
  waiting for transfers between devices: 138 us -> 45.4 us
  matrix products: 46.4 us -> 0 us
  Pallas kernels: 0 us -> 42.2 us
  between operations: 0.7 us -> 14.3 us
  starting transfers between devices: 21.5 us -> 10.2 us
    another operation x10 -> x0, other arithmetic: 349 us -> none  [the longest x4 189 us: per_device(): factor = jnp.linalg.cholesky(normal)]
    scatter x33 -> x0, local copies, waits for them, and re-layouts: 259 us -> none
    all_to_all x4 -> x2, waiting for transfers between devices: 138 us -> 0.01 us  [the longest x1 0.01 us: per_device(): lax.all_to_all(projected, 'freq', split_axis=0, concat_axis=0, tiled=True)]
    scatter x32 -> x0, other arithmetic: 98.1 us -> none
    all_gather x0 -> x1, blocking collectives: none -> 53.5 us  [per_device(): lax.all_gather(weight.astype(bf16), 'freq', axis=1, tiled=True)]
    all_gather x0 -> x1, waiting for transfers between devices: none -> 45.4 us  [per_device(): coefficients = lax.all_gather(coefficients, 'freq')]
    pallas_call x0 -> x4, Pallas kernels: none -> 42.2 us  [the longest x1 17 us: per_device(): pl.pallas_call(functools.partial(filter_kernel, shards), grid=(items,), i...]
    dot_general x5 -> x0, matrix products: 39 us -> none  [the longest x1 15.2 us: per_device(): jnp.dot(spectra.reshape(base_count * chan_local, 2 * length), inverse, pr...]
  transfers between devices with their start and end apart: 4 -> 3, of which waited for: 1 -> 1; matrix products, arithmetic and copies ran while one was open for 83% -> 2% of each run, Pallas kernels for 0% -> 4%
where the time goes in v1:
time: 263 us; the launch traced here: 262 us
  blocking collectives  112 us (43%)
  waiting for transfers between devices  45.4 us (17%)
  Pallas kernels  42.2 us (16%)
  local copies, waits for them, and re-layouts  29.6 us (11%)
  between operations  14.3 us (5%)
  starting transfers between devices  10.2 us (4%)
  other arithmetic  9.15 us (3%)
    all_gather x1, blocking collectives, per_device(): lax.all_gather(weight.astype(bf16), 'freq', axis=1, tiled=True)  53.5 us
    all_gather x1, waiting for transfers between devices, per_device(): coefficients = lax.all_gather(coefficients, 'freq')  45.4 us
    unnamed x1, blocking collectives  35.5 us
    all_to_all x1, blocking collectives, per_device(): lax.all_to_all(jnp.transpose(mean, (1, 0, 2, 3)), 'freq', split_axis=0, c...  22.6 us
    pallas_call x1, Pallas kernels, per_device(): pl.pallas_call(functools.partial(filter_kernel, shards), grid=(items,), i...  17 us
    slice x1, local copies, waits for them, and re-layouts, per_device(): vis[:, :, 1, :]  13.8 us
    pallas_call x1, Pallas kernels, per_device(): pl.pallas_call(clean_kernel, grid_spec=pltpu.PrefetchScalarGridSpec(num_s...  13.5 us
    pallas_call x1, Pallas kernels, per_device(): pl.pallas_call(functools.partial(inverse_kernel, batch, ridge, newton_sca...  9.39 us
  transfers between devices with their start and end apart: 3, of which 1 were waited for; matrix products, arithmetic and copies ran while one was open for 2% of the time, Pallas kernels for 4%

profile of v1, /device:TPU:0, one launch (start us, length us, event | category | flops | bytes accessed | tf_op | source)
XLA Modules:
  0.0 262.5 jit_solution(8100926587440077085)
XLA Ops:
  6.5 1.1 fusion.21
  7.6 1.0 fusion.23
  8.7 13.8 %fusion.28 = (bf16[16,384,1,256]{3,2,1,0:T(2,128)(2,1)}, bf16[16,384,1,256]{3,2,1,0:T(2,128)(2,1)}) fusion(bf16[16,384,2,256]{3,2,1,0:T(2,128)(2,1)} %param.4), kind=kLoop, calls=%fused_computation.50 | loop fusion | bytes 12582912 | tf_op jit(solution)/shard_map/slice | solution.py:192
  22.6 0.1 add_multiply_fusion
  22.8 3.1 %fusion.3 = bf16[1536,128]{0,1:T(8,128)(2,1)S(1)} fusion(s32[1536]{0:T(1024)S(1)} %multiply_add_fusion), kind=kLoop, calls=%fused_computation.10 | loop fusion | flops 1966080 | bytes 399360 | tf_op jit(solution)/shard_map/convert_element_type | solution.py:46
  25.9 0.1 copy.35.basis_ref
  26.0 8.7 %copy_bitcast_fusion = (bf16[16,384,256]{2,1,0:T(8,128)(2,1)}, bf16[16,384,256]{2,1,0:T(8,128)(2,1)}) fusion(bf16[16,384,1,256]{3,2,1,0:T(2,128)(2,1)} %get-tuple-element.9, bf16[16,384,1,256]{3,2,1,0:T(2,128)(2,1)} %get-tuple-element.10), kind=kLoop, calls=%fused_computation.1 | loop fusion | bytes 12582912 | tf_op jit(solution)/shard_map/squeeze | solution.py:192
  34.8 17.0 %shard_map.46 = (bf16[16,512,384]{2,1,0:T(8,128)(2,1)}, bf16[4,16,128,128]{3,2,1,0:T(8,128)(2,1)S(1)}) custom-call(bf16[16,384,256]{2,1,0:T(8,128)(2,1)} %get-tuple-element.14.re_ref, bf16[16,384,256]{2,1,0:T(8,128)(2,1)} %get-tuple-element.13.im_ref, bf16[512,512]{1,0:T(8,128)(2,1)S(1)} %maximum_convert_fusion.fwd_ref, bf16[512,512]{1,0:T(8,128)(2,1)S(1)} %bitcast.21, ...), custom_call_target="tpu_custom_call" | custom-call | flops 6442450944 | bytes 12582912 | tf_op jit(solution)/shard_map/pallas_call | solution.py:175
  51.7 1.3 copy-done.1
  53.1 6.3 %all-to-all-start = ((bf16[4,16,128,128]{3,2,1,0:T(8,128)(2,1)}), bf16[4,16,128,128]{3,2,1,0:T(8,128)(2,1)S(1)}, u32[]{:S(2)}, u32[]{:S(2)}) async-start(bf16[4,16,128,128]{3,2,1,0:T(8,128)(2,1)} %copy-done.1), calls=%async_computation | async-start | bytes 4194304 | tf_op jit(solution)/shard_map/all_to_all | solution.py:211
  59.4 0.2 copy.37.basis_ref
  59.6 53.5 %all_gather.12 = bf16[16,1536]{1,0:T(8,128)(2,1)S(1)} all-gather(bf16[16,384]{1,0:T(8,128)(2,1)S(1)} %get-tuple-element.11), channel_id=1, replica_groups=mesh['win'=2,'bl'=4,'freq'=4] {'freq'}, dimensions={1}, use_global_device_ids=true | all-gather | bytes 61440 | tf_op jit(solution)/shard_map/all_gather | solution.py:172
  113.1 0.1 copy.36.weight_ref
  113.2 3.1 %fusion.7.basis_t_ref = bf16[128,1536]{1,0:T(8,128)(2,1)S(1)} fusion(s32[1536]{0:T(1024)S(1)} %multiply_add_fusion), kind=kLoop, calls=%fused_computation.14 | loop fusion | flops 1966080 | bytes 399360 | tf_op jit(solution)/shard_map/convert_element_type | solution.py:46
  116.3 9.4 %shard_map.47.inverse_ref = f32[16,128,128]{2,1,0:T(8,128)S(1)} custom-call(bf16[16,1,1536]{2,1,0:T(2,128)(2,1)S(1)} %copy.36.weight_ref, bf16[1536,128]{1,0:T(8,128)(2,1)S(1)} %copy.37.basis_ref, bf16[128,1536]{1,0:T(8,128)(2,1)S(1)} %fusion.7.basis_t_ref), custom_call_target="tpu_custom_call" | custom-call | flops 20000000000 | bytes 1048576 | tf_op jit(solution)/shard_map/pallas_call | solution.py:197
  125.7 2.3 shard_map.48
  128.0 0.0 all-gather.3.cloned.1.call-update
  128.0 0.9 fusion.29.basis_t_ref
  128.9 45.4 %all-gather.3.cloned.1.call-done = bf16[64,128,128]{2,1,0:T(8,128)(2,1)} async-done(((bf16[16,128,128]{2,1,0:T(8,128)(2,1)}), bf16[64,128,128]{2,1,0:T(8,128)(2,1)}) %all-gather.3.cloned.1.call-update) | async-done | bytes 2097168 | tf_op jit(solution)/shard_map/all_gather | solution.py:220
  174.4 1.6 copy-done
  176.0 13.5 %shard_map.49 = bf16[8,512,384]{2,1,0:T(8,128)(2,1)} custom-call(s32[16]{0:T(128)S(1)} %copy-done.4, bf16[16,512,384]{2,1,0:T(8,128)(2,1)} %get-tuple-element.7.fringe_ref, bf16[4,16,128,128]{3,2,1,0:T(8,128)(2,1)S(1)} %bitcast.19, bf16[128,384]{1,0:T(8,128)(2,1)S(1)} %fusion.29.basis_t_ref, f32[16,1,384]{2,1,0:T(1,128)S(1)} %copy-done.3), custom_call_target="tpu_custom_call" | custom-call | tf_op jit(solution)/shard_map/pallas_call | solution.py:222
  189.5 3.8 %all-to-all-start.1 = ((bf16[8,512,384]{2,1,0:T(8,128)(2,1)}), bf16[8,512,384]{2,1,0:T(8,128)(2,1)S(1)}, u32[]{:S(2)}, u32[]{:S(2)}) async-start(bf16[8,512,384]{2,1,0:T(8,128)(2,1)} %shard_map.49), calls=%async_computation.1 | async-start | bytes 6291456 | tf_op jit(solution)/shard_map/all_to_all | solution.py:238
  193.4 0.6 dynamic-slice
  194.6 0.2 dynamic-update-slice
  194.8 35.5 %all-reduce = s32[64]{0:T(128)S(1)} all-reduce(s32[64]{0:T(128)S(1)} %dynamic-update-slice), channel_id=1, replica_groups=mesh['win'=2,'bl'=4,'freq'=4] {'bl'}, use_global_device_ids=true, to_apply=%add | all-reduce | flops 64 | bytes 512
  230.3 0.1 fusion.26
  230.5 0.4 convert_reduce_fusion
  230.9 0.2 fusion.12
  231.1 0.1 copy.38
  231.2 22.6 %all_to_all.15 = bf16[4,2,128,384]{3,2,1,0:T(8,128)(2,1)S(1)} all-to-all(bf16[4,2,128,384]{3,2,1,0:T(8,128)(2,1)S(1)} %copy.38), channel_id=1, replica_groups=mesh['win'=2,'bl'=4,'freq'=4] {'freq'}, dimensions={0} | all-to-all | bytes 1572864 | tf_op jit(solution)/shard_map/all_to_all | solution.py:244
  253.8 0.6 copy.39
  254.5 1.2 reshape.47
  (32 shorter events, 0.2 us)
Async XLA Ops:
  8.7 13.9 %copy-start.7 = (s32[16]{0:T(128)S(1)}, s32[16]{0:T(128)}, u32[]{:S(2)}) copy-start(s32[16]{0:T(128)} %param.6) | copy-start | bytes 196
  8.7 14.0 %copy-start.6 = (s32[16,384]{1,0:T(8,128)S(1)}, s32[16,384]{1,0:T(8,128)}, u32[]{:S(2)}) copy-start(s32[16,384]{1,0:T(8,128)} %param.5) | copy-start | bytes 73732
  22.8 12.0 %copy-start.2 = (f32[16,1,384]{2,1,0:T(1,128)}, f32[16,1,384]{2,1,0:T(1,128)S(1)}, u32[]{:S(2)}) copy-start(f32[16,1,384]{2,1,0:T(1,128)S(1)} %reshape.45.weight_ref) | copy-start | bytes 73732
  25.8 33.5 %copy-start.5 = (bf16[1536,128]{0,1:T(8,128)(2,1)}, bf16[1536,128]{0,1:T(8,128)(2,1)S(1)}, u32[]{:S(2)}) copy-start(bf16[1536,128]{0,1:T(8,128)(2,1)S(1)} %fusion.3) | copy-start | bytes 1179652
  51.7 1.3 copy-start.1
  53.1 72.6 %all-to-all-start = ((bf16[4,16,128,128]{3,2,1,0:T(8,128)(2,1)}), bf16[4,16,128,128]{3,2,1,0:T(8,128)(2,1)S(1)}, u32[]{:S(2)}, u32[]{:S(2)}) async-start(bf16[4,16,128,128]{3,2,1,0:T(8,128)(2,1)} %copy-done.1), calls=%async_computation | async-start | bytes 4194304 | tf_op jit(solution)/shard_map/all_to_all | solution.py:211
  59.4 115.0 %all-gather.3.cloned.1.call-start = ((), (), s32[]{:S(2)}) async-start(), calls=%async_computation.3 | async-start | bytes 2621440 | tf_op jit(solution)/shard_map/all_gather | solution.py:220
  125.7 48.7 %copy-start.3 = (f32[16,1,384]{2,1,0:T(1,128)S(1)}, f32[16,1,384]{2,1,0:T(1,128)}, u32[]{:S(2)}) copy-start(f32[16,1,384]{2,1,0:T(1,128)} %copy-done.2) | copy-start | bytes 73732
  125.7 48.7 %copy-start.4 = (s32[16]{0:T(128)S(1)}, s32[16]{0:T(128)}, u32[]{:S(2)}) copy-start(s32[16]{0:T(128)} %ids_ref.1) | copy-start | bytes 196
  174.4 1.6 copy-start
  189.5 3.9 %copy-start.8 = (u32[32]{0:T(128)S(1)}, u32[32]{0:T(128)}, u32[]{:S(2)}) copy-start(u32[32]{0:T(128)} %constant.74) | copy-start | bytes 388
  189.5 41.0 %all-to-all-start.1 = ((bf16[8,512,384]{2,1,0:T(8,128)(2,1)}), bf16[8,512,384]{2,1,0:T(8,128)(2,1)S(1)}, u32[]{:S(2)}, u32[]{:S(2)}) async-start(bf16[8,512,384]{2,1,0:T(8,128)(2,1)} %shard_map.49), calls=%async_computation.1 | async-start | bytes 6291456 | tf_op jit(solution)/shard_map/all_to_all | solution.py:238
Sparse Core Ops, SparseCore 0:
  128.2 46.1 all-gather.2

commit v2 on v1

v2 whole, which is shorter than its diff:
```python
import functools
import math

import jax
import jax.numpy as jnp
import numpy as np
from jax import lax
from jax.experimental import pallas as pl
from jax.experimental.pallas import tpu as pltpu
from jax.sharding import PartitionSpec as P

CH = 1536
DELAYS = 128
NBAND = 8
GPO = 2
CAP = 8


def fourier_tables(length):
    sample_index = np.arange(length, dtype=np.int32)
    phase_index = sample_index[:, None] * sample_index[None, :] % length
    angles = phase_index.astype(np.float32) * np.float32(2.0 * math.pi / length)
    cosine = np.cos(angles)
    sine_table = np.sin(angles)
    forward = np.concatenate(
        [np.concatenate([cosine, -sine_table], 1), np.concatenate([sine_table, cosine], 1)], 0
    )
    return forward.astype(jnp.bfloat16)


def band_response(band, length, band_count):
    mode_index = jnp.arange(length, dtype=jnp.int32)
    signed_modes = (mode_index - length * (mode_index >= length // 2).astype(jnp.int32)).astype(
        jnp.float32
    )
    center = (band.astype(jnp.float32) - (band_count - 1) / 2.0) * (length / (4.0 * band_count))
    band_width = length / 32.0
    offset_ratio = (signed_modes[None, :] - center[:, None]) / band_width
    single = (0.15 + 0.85 / (1.0 + offset_ratio**4)) / length
    return jnp.concatenate([single, single], 1)


def make_basis(channels, modes):
    channel_index = np.arange(channels, dtype=np.int32)
    order_index = np.arange(modes, dtype=np.int32)
    phase_index = order_index[None, :] * (2 * channel_index[:, None] + 1) % (4 * channels)
    return np.cos(phase_index.astype(np.float32) * np.float32(math.pi / (2 * channels))).astype(
        jnp.bfloat16
    )


NT = (((1,), (1,)), ((), ()))
BIG = 48 * 1024 * 1024


def dot32(left, right):
    return jnp.dot(left, right, preferred_element_type=jnp.float32)


def halves(value):
    high = value.astype(jnp.bfloat16)
    return high, (value - high.astype(jnp.float32)).astype(jnp.bfloat16)


def dot_split(left, right):
    left_high, left_low = left
    right_high, right_low = right
    return dot32(left_high, right_high) + (
        dot32(left_high, right_low) + dot32(left_low, right_high)
    )


def filter_kernel(shards, chunks, vis_ref, fwd_ref, inv_ref, resp_ref, weight_ref, basis_ref,
                  fringe_ref, proj_ref):
    batch, half = vis_ref.shape[0], vis_ref.shape[3]
    spectra = [
        dot32(vis_ref[i, :, 0, :], fwd_ref[:half]) + dot32(vis_ref[i, :, 1, :], fwd_ref[half:])
        for i in range(batch)
    ]
    spectra = [(spectra[i] * resp_ref[i]).astype(jnp.bfloat16) for i in range(batch)]
    for i in range(batch):
        fringe = lax.dot_general(inv_ref[...], spectra[i], NT, preferred_element_type=jnp.float32)
        fringe = (fringe * weight_ref[i]).astype(jnp.bfloat16)
        fringe_ref[i] = fringe
        projected = dot32(fringe, basis_ref[...])
        size = projected.shape[0] // chunks
        for h in range(chunks):
            piece = projected[h * size:(h + 1) * size].reshape(shards, -1, projected.shape[1])
            proj_ref[:, i, h] = piece.astype(jnp.bfloat16)


def inverse_kernel(batch, ridge, scales, start, weight_ref, basis_ref, basis_t_ref, out_ref):
    modes = out_ref.shape[1]
    eye = (
        lax.broadcasted_iota(jnp.int32, (modes, modes), 0)
        == lax.broadcasted_iota(jnp.int32, (modes, modes), 1)
    ).astype(jnp.float32)
    normals = [
        dot32(basis_t_ref[...] * weight_ref[i], basis_ref[...]) + ridge * eye for i in range(batch)
    ]
    first = scales[0]
    guess = [first * (2.0 * start * eye - start * start * normal) for normal in normals]
    normals = [halves(normal) for normal in normals]
    for scale in scales[1:]:
        guess_parts = [halves(value) for value in guess]
        product = [dot_split(n, g) for n, g in zip(normals, guess_parts)]
        change = [halves(2.0 * eye - value) for value in product]
        guess = [scale * dot_split(g, c) for g, c in zip(guess_parts, change)]
    for i in range(batch):
        out_ref[i] = guess[i]


def solve_kernel(batch, recv_ref, inverse_ref, *out_refs):
    for i in range(batch):
        inverse = halves(inverse_ref[i])
        for h, out_ref in enumerate(out_refs):
            total = jnp.sum(recv_ref[:, i, h].astype(jnp.float32), axis=0)
            out_ref[i] = dot_split(halves(total), inverse).astype(jnp.bfloat16)


def clean_kernel(ids_ref, fringe_ref, coef_ref, basis_t_ref, weight_ref, out_ref, total_ref):
    item = pl.program_id(0)

    @pl.when(item == 0)
    def _():
        total_ref[...] = jnp.zeros_like(total_ref)

    batch, size = fringe_ref.shape[0], fringe_ref.shape[1]
    for i in range(batch):
        coef = coef_ref[:, i].astype(jnp.float32)
        coef = coef.reshape(-1, coef.shape[2]).astype(jnp.bfloat16)
        fitted = dot32(coef, basis_t_ref[...]) * weight_ref[i]
        group = ids_ref[item * batch + i]
        total_ref[group, :size] += fringe_ref[i].astype(jnp.float32) - fitted
        total_ref[group, size:] += jnp.ones_like(total_ref[group, size:])

    @pl.when(item == pl.num_programs(0) - 1)
    def _():
        out_ref[...] = total_ref[...].astype(jnp.bfloat16)


def newton_scales(low, high):
    scales = []
    value = (high + low) / (high - low)
    while True:
        doubled = 2.0 * value * value
        scales.append(doubled / (doubled - 1.0))
        value = doubled - 1.0
        if value > 1e6:
            return scales


def full(shape):
    return pl.BlockSpec(shape, lambda i, *rest: (0,) * len(shape))


def lead(shape):
    return pl.BlockSpec(shape, lambda i, *rest: (i,) + (0,) * (len(shape) - 1))


def second(shape):
    return pl.BlockSpec(shape, lambda i, *rest: (0, i) + (0,) * (len(shape) - 2))


def per_device(vis, flags, band, group_id):
    items, chan, _, length = vis.shape
    both = 2 * length
    shards = lax.axis_size("freq")
    owners = lax.axis_size("bl")
    groups = GPO * owners
    time_local = length // shards
    rows = 2 * time_local
    pair = 2 if items % 2 == 0 else 1
    chunks = 2 if rows % 32 == 0 else 1
    rows //= chunks
    size = both // chunks
    bf16, f32 = jnp.bfloat16, jnp.float32

    table = fourier_tables(length)
    forward = jnp.asarray(table)
    inverse_t = forward
    if chunks == 1:
        inverse_t = table.reshape(2, shards, time_local, both)
        inverse_t = jnp.asarray(np.transpose(inverse_t, (1, 0, 2, 3)).reshape(both, both))
    response = band_response(band, length, NBAND).reshape(items, 1, both)
    basis = make_basis(CH, DELAYS)
    basis_t = jnp.asarray(basis.T.copy())
    basis = jnp.asarray(basis)
    basis_local = lax.dynamic_slice_in_dim(basis, lax.axis_index("freq") * chan, chan, 0)
    weight = 1.0 - flags.astype(f32)
    weight_rows = weight.reshape(items, 1, chan)
    weight_half = weight.astype(bf16)
    if shards <= 8:
        pieces = [weight_half] + [
            lax.ppermute(weight_half, "freq", [(d, (d - j) % shards) for d in range(shards)])
            for j in range(1, shards)
        ]
        doubled = jnp.concatenate(pieces + pieces, axis=1)
        offset = (shards - lax.axis_index("freq")) % shards * chan
        weight_full = lax.dynamic_slice_in_dim(doubled, offset, CH, 1)
    else:
        weight_full = lax.all_gather(weight_half, "freq", axis=1, tiled=True)
        response, weight_full = lax.optimization_barrier((response, weight_full))
    weight_full = weight_full.reshape(items, 1, CH)

    fringe, projected = pl.pallas_call(
        functools.partial(filter_kernel, shards, chunks),
        grid=(items // pair,),
        in_specs=[
            lead((pair, chan, 2, length)), full((both, both)), full((both, both)),
            lead((pair, 1, both)), lead((pair, 1, chan)), full((chan, DELAYS)),
        ],
        out_specs=[lead((pair, both, chan)), second((shards, pair, chunks, rows, DELAYS))],
        out_shape=[
            jax.ShapeDtypeStruct((items, both, chan), bf16),
            jax.ShapeDtypeStruct((shards, items, chunks, rows, DELAYS), bf16),
        ],
        compiler_params=pltpu.CompilerParams(vmem_limit_bytes=BIG),
        cost_estimate=pl.CostEstimate(
            flops=4 * items * chan * both * both, bytes_accessed=4 * items * chan * both,
            transcendentals=0,
        ),
    )(vis, forward, inverse_t, response, weight_rows, basis_local)

    projected, weight_full = lax.optimization_barrier((projected, weight_full))
    ridge = CH / 64.0
    high = ridge + 1.05 * CH
    batch = 4 if items % 4 == 0 else 1
    inverse = pl.pallas_call(
        functools.partial(
            inverse_kernel, batch, ridge, newton_scales(ridge, high), 2.0 / (ridge + high)
        ),
        grid=(items // batch,),
        in_specs=[lead((batch, 1, CH)), full((CH, DELAYS)), full((DELAYS, CH))],
        out_specs=lead((batch, DELAYS, DELAYS)),
        out_shape=jax.ShapeDtypeStruct((items, DELAYS, DELAYS), f32),
        compiler_params=pltpu.CompilerParams(vmem_limit_bytes=BIG),
        cost_estimate=pl.CostEstimate(
            flops=20_000_000_000, bytes_accessed=4 * items * DELAYS * DELAYS, transcendentals=0
        ),
    )(weight_full, basis, basis_t)

    received = lax.all_to_all(projected, "freq", split_axis=0, concat_axis=0, tiled=True)
    coefficients = pl.pallas_call(
        functools.partial(solve_kernel, batch),
        grid=(items // batch,),
        in_specs=[
            second((shards, batch, chunks, rows, DELAYS)), lead((batch, DELAYS, DELAYS)),
        ],
        out_specs=[lead((batch, rows, DELAYS))] * chunks,
        out_shape=[jax.ShapeDtypeStruct((items, rows, DELAYS), bf16)] * chunks,
        compiler_params=pltpu.CompilerParams(vmem_limit_bytes=BIG),
    )(received, inverse)
    basis_local_t = basis_local.T
    tall = size + 16

    def clean(h, gathered):
        return pl.pallas_call(
            clean_kernel,
            grid_spec=pltpu.PrefetchScalarGridSpec(
                num_scalar_prefetch=1,
                grid=(items // batch,),
                in_specs=[
                    pl.BlockSpec((batch, size, chan), lambda i, ids: (i, h, 0)),
                    second((shards, batch, rows, DELAYS)), full((DELAYS, chan)),
                    lead((batch, 1, chan)),
                ],
                out_specs=full((groups, tall, chan)),
                scratch_shapes=[pltpu.VMEM((groups, tall, chan), f32)],
            ),
            out_shape=jax.ShapeDtypeStruct((groups, tall, chan), bf16),
            compiler_params=pltpu.CompilerParams(vmem_limit_bytes=BIG),
            cost_estimate=pl.CostEstimate(
                flops=2_000_000_000, bytes_accessed=4 * items * size * chan, transcendentals=0
            ),
        )(group_id, fringe, gathered, basis_local_t, weight_rows)

    gathered = [lax.all_gather(part, "freq") for part in coefficients]
    pieces = []
    for h in range(chunks):
        sums = clean(h, gathered[h])
        arrived = lax.all_to_all(sums, "bl", split_axis=0, concat_axis=0, tiled=True)
        total = jnp.sum(arrived.reshape(owners, GPO, tall, chan).astype(f32), 0)
        counts = jnp.maximum(total[:, size:size + 1, :1], 1.0)
        mean = (total[:, :size] / counts).astype(bf16).reshape(GPO, shards, rows, chan)
        pieces.append(jnp.transpose(mean, (1, 0, 2, 3)))
    means = jnp.stack(pieces, 1)
    swapped = lax.all_to_all(means, "freq", split_axis=0, concat_axis=0, tiled=True)
    averaged = jnp.transpose(swapped, (2, 1, 3, 0, 4))
    return averaged.reshape(GPO, 2, time_local, CH)


def solution(mesh):
    in_specs = (P("bl", "freq", None, "win"), P("bl", "freq"), P("bl"), P("bl"))
    out_specs = P("bl", None, ("win", "freq"), None)
    return jax.shard_map(
        per_device, mesh=mesh, in_specs=in_specs, out_specs=out_specs, check_vma=False
    )
```

time: 263 us -> 217 us (0.83)
  blocking collectives: 112 us -> 22.9 us
  waiting for transfers between devices: 45.4 us -> 103 us
  local copies, waits for them, and re-layouts: 29.6 us -> 9.11 us
  starting transfers between devices: 10.2 us -> 17.4 us
  other arithmetic: 9.15 us -> 3.3 us
  Pallas kernels: 42.2 us -> 46.8 us
    all_gather x1 -> x0, blocking collectives: 53.5 us -> none  [per_device(): lax.all_gather(weight.astype(bf16), 'freq', axis=1, tiled=True)]
    all_to_all x1, waiting for transfers between devices: 0.01 us -> 36.2 us  [per_device(): lax.all_to_all(projected, 'freq', split_axis=0, concat_axis=0, tiled=True)]
    unnamed x1 -> x0, blocking collectives: 35.5 us -> none
    all_to_all x1 -> x2, waiting for transfers between devices: 0.01 us -> 20.6 us  [per_device(): lax.all_to_all(sums, 'bl', split_axis=0, concat_axis=0, tiled=True)]
    slice x1 -> x0, local copies, waits for them, and re-layouts: 13.8 us -> none  [per_device(): vis[:, :, 1, :]]
    squeeze x1 -> x0, local copies, waits for them, and re-layouts: 8.73 us -> none  [per_device(): vis[:, :, 1, :]]
    ppermute x0 -> x3, starting transfers between devices: none -> 6.06 us  [per_device(): lax.ppermute(weight_half, 'freq', [(d, (d - j) % shards) for d in range(s...]
    convert_element_type x4 -> x2, other arithmetic: 6.18 us -> 0.26 us  [per_device(): (total[:, :size] / counts).astype(bf16).reshape(GPO, shards, rows, chan)]
  transfers between devices with their start and end apart: 3 -> 8, of which waited for: 1 -> 4; matrix products, arithmetic and copies ran while one was open for 2% -> 1% of each run, Pallas kernels for 4% -> 21%
where the time goes in v2:
time: 217 us; the launch traced here: 216 us
  waiting for transfers between devices  103 us (47%)
  Pallas kernels  46.8 us (22%)
  blocking collectives  22.9 us (11%)
  starting transfers between devices  17.4 us (8%)
  between operations  13.6 us (6%)
  local copies, waits for them, and re-layouts  9.11 us (4%)
  other arithmetic  3.3 us (2%)
    all_gather x2, waiting for transfers between devices, per_device(): gathered = [lax.all_gather(part, 'freq') for part in coefficients]  45.2 us
    all_to_all x1, waiting for transfers between devices, per_device(): lax.all_to_all(projected, 'freq', split_axis=0, concat_axis=0, tiled=True)  36.2 us
    pallas_call x1, Pallas kernels, per_device(): pl.pallas_call(functools.partial(filter_kernel, shards, chunks), grid=(it...  23.5 us
    all_to_all x1, blocking collectives, per_device(): lax.all_to_all(means, 'freq', split_axis=0, concat_axis=0, tiled=True)  22.9 us
    all_to_all x2, waiting for transfers between devices, per_device(): lax.all_to_all(sums, 'bl', split_axis=0, concat_axis=0, tiled=True)  20.6 us
    pallas_call x2, Pallas kernels, clean(): pl.pallas_call(clean_kernel, grid_spec=pltpu.PrefetchScalarGridSpec(num_s...  11.5 us
    pallas_call x1, Pallas kernels, per_device(): pl.pallas_call(functools.partial(inverse_kernel, batch, ridge, newton_sca...  9.37 us
    all_to_all x2, starting transfers between devices, per_device(): lax.all_to_all(sums, 'bl', split_axis=0, concat_axis=0, tiled=True)  7.16 us
  transfers between devices with their start and end apart: 8, of which 4 were waited for; matrix products, arithmetic and copies ran while one was open for 1% of the time, Pallas kernels for 21%

profile of v2, /device:TPU:0, one launch (start us, length us, event | category | flops | bytes accessed | tf_op | source)
XLA Modules:
  0.0 215.7 jit_solution(14066190923170986726)
XLA Ops:
  6.5 0.7 constant_dynamic-update-slice_fusion.7
  7.3 5.0 %collective-permute-start = (bf16[16,384]{1,0:T(8,128)(2,1)S(1)}, bf16[16,384]{1,0:T(8,128)(2,1)S(1)}, u32[]{:S(2)}, u32[]{:S(2)}) collective-permute-start(bf16[16,384]{1,0:T(8,128)(2,1)S(1)} %get-tuple-element.18), channel_id=1, source_target_pairs={{0,3},{1,0},{2,1},{3,2},{4,7},{5,4},{6,5},{7,6},{8,11},{9,8},{10,9... | collective-permute-start | bytes 36872 | tf_op jit(solution)/shard_map/ppermute | solution.py:195
  12.3 1.0 collective-permute-start.2
  13.3 0.7 convert_subtract_fusion
  14.1 0.7 add_multiply_fusion.1
  14.9 0.9 dynamic-slice_bitcast_fusion.1
  15.8 0.1 copy.22.basis_ref
  16.0 1.0 copy-done.4
  17.0 23.5 %shard_map.73 = (bf16[16,512,384]{2,1,0:T(8,128)(2,1)}, bf16[4,16,2,64,128]{4,3,2,1,0:T(8,128)(2,1)S(1)}) custom-call(bf16[16,384,2,256]{3,2,1,0:T(2,128)(2,1)} %vis_ref.1, bf16[512,512]{1,0:T(8,128)(2,1)S(1)} %copy-done.4, bf16[512,512]{1,0:T(8,128)(2,1)S(1)} %copy-done.4, f32[16,1,512]{2,1,0:T(1,128)S(1)} %reshape.33.resp_ref, ...), custom_call_target="tpu_custom_call" | custom-call | flops 6442450944 | bytes 12582912 | tf_op jit(solution)/shard_map/pallas_call | solution.py:206
  40.5 1.3 copy-done
  42.0 4.1 %all-to-all-start = ((bf16[4,16,2,64,128]{4,3,2,1,0:T(8,128)(2,1)}), bf16[4,16,2,64,128]{4,3,2,1,0:T(8,128)(2,1)S(1)}, u32[]{:S(2)}, u32[]{:S(2)}) async-start(bf16[4,16,2,64,128]{4,3,2,1,0:T(8,128)(2,1)} %copy-done), calls=%async_computation | async-start | bytes 4194304 | tf_op jit(solution)/shard_map/all_to_all | solution.py:243
  46.2 1.0 copy-done.5
  47.2 1.0 copy-done.6
  48.2 9.4 %shard_map.74.inverse_ref = f32[16,128,128]{2,1,0:T(8,128)S(1)} custom-call(bf16[16,1,1536]{2,1,0:T(2,128)(2,1)S(1)} %copy.23.weight_ref, bf16[1536,128]{1,0:T(8,128)(2,1)S(1)} %copy-done.5, bf16[128,1536]{1,0:T(8,128)(2,1)S(1)} %copy-done.6), custom_call_target="tpu_custom_call" | custom-call | flops 20000000000 | bytes 1048576 | tf_op jit(solution)/shard_map/pallas_call | solution.py:229
  57.5 36.2 %all-to-all-done.recv_ref = bf16[4,16,2,64,128]{4,3,2,1,0:T(8,128)(2,1)S(1)} async-done(((bf16[4,16,2,64,128]{4,3,2,1,0:T(8,128)(2,1)}), bf16[4,16,2,64,128]{4,3,2,1,0:T(8,128)(2,1)S(1)}, u32[]{:S(2)}, u32[]{:S(2)}) %all-to-all-start) | async-done | bytes 2097184 | tf_op jit(solution)/shard_map/all_to_all | solution.py:243
  93.7 2.4 %shard_map.75 = (bf16[16,64,128]{2,1,0:T(8,128)(2,1)}, bf16[16,64,128]{2,1,0:T(8,128)(2,1)}) custom-call(bf16[4,16,2,64,128]{4,3,2,1,0:T(8,128)(2,1)S(1)} %all-to-all-done.recv_ref, f32[16,128,128]{2,1,0:T(8,128)S(1)} %shard_map.74.inverse_ref), custom_call_target="tpu_custom_call" | custom-call | tf_op jit(solution)/shard_map/pallas_call | solution.py:244
  96.2 0.7 all-gather.5.cloned.1.call-update
  96.9 26.7 %all-gather.7.cloned.1.call-done = bf16[64,64,128]{2,1,0:T(8,128)(2,1)} async-done(((bf16[16,64,128]{2,1,0:T(8,128)(2,1)}), bf16[64,64,128]{2,1,0:T(8,128)(2,1)}) %all-gather.7.cloned.1.call-update) | async-done | bytes 1048592 | tf_op jit(solution)/shard_map/all_gather | solution.py:278
  123.6 1.2 copy-done.2
  124.8 5.7 %shard_map.77 = bf16[8,272,384]{2,1,0:T(8,128)(2,1)} custom-call(s32[16]{0:T(128)S(1)} %copy-done.3, bf16[16,512,384]{2,1,0:T(8,128)(2,1)} %get-tuple-element.11.fringe_ref, bf16[4,16,64,128]{3,2,1,0:T(8,128)(2,1)S(1)} %bitcast.24, bf16[128,384]{1,0:T(8,128)(2,1)S(1)} %get-tuple-element.19.basis_t_ref, f32[16,1,384]{2,1,0:T(1,128)S(1)} %reshape.34.weight_ref), custom_call_target="tpu_custom_call" | custom-call | flops 2000000000 | bytes 6291456 | tf_op jit(solution)/shard_map/pallas_call | solution.py:258
  130.5 3.6 %all-to-all-start.2 = ((bf16[8,272,384]{2,1,0:T(8,128)(2,1)}), bf16[8,272,384]{2,1,0:T(8,128)(2,1)S(1)}, u32[]{:S(2)}, u32[]{:S(2)}) async-start(bf16[8,272,384]{2,1,0:T(8,128)(2,1)} %shard_map.77), calls=%async_computation.2 | async-start | bytes 3342336 | tf_op jit(solution)/shard_map/all_to_all | solution.py:282
  134.1 18.5 %all-gather.5.cloned.1.call-done = bf16[64,64,128]{2,1,0:T(8,128)(2,1)} async-done(((bf16[16,64,128]{2,1,0:T(8,128)(2,1)}), bf16[64,64,128]{2,1,0:T(8,128)(2,1)}) %all-gather.5.cloned.1.call-update) | async-done | bytes 1048592 | tf_op jit(solution)/shard_map/all_gather | solution.py:278
  152.6 1.2 copy-done.1
  153.8 5.8 %shard_map.76 = bf16[8,272,384]{2,1,0:T(8,128)(2,1)} custom-call(s32[16]{0:T(128)S(1)} %copy-done.3, bf16[16,512,384]{2,1,0:T(8,128)(2,1)} %get-tuple-element.11.fringe_ref, bf16[4,16,64,128]{3,2,1,0:T(8,128)(2,1)S(1)} %bitcast.23, bf16[128,384]{1,0:T(8,128)(2,1)S(1)} %get-tuple-element.19.basis_t_ref, f32[16,1,384]{2,1,0:T(1,128)S(1)} %reshape.34.weight_ref), custom_call_target="tpu_custom_call" | custom-call | flops 2000000000 | bytes 6291456 | tf_op jit(solution)/shard_map/pallas_call | solution.py:258
  159.6 3.6 %all-to-all-start.1 = ((bf16[8,272,384]{2,1,0:T(8,128)(2,1)}), bf16[8,272,384]{2,1,0:T(8,128)(2,1)S(1)}, u32[]{:S(2)}, u32[]{:S(2)}) async-start(bf16[8,272,384]{2,1,0:T(8,128)(2,1)} %shard_map.76), calls=%async_computation.1 | async-start | bytes 3342336 | tf_op jit(solution)/shard_map/all_to_all | solution.py:282
  163.2 0.3 convert_reduce_fusion
  163.6 0.1 fusion
  163.7 20.6 %all-to-all-done.1 = bf16[8,272,384]{2,1,0:T(8,128)(2,1)S(1)} async-done(((bf16[8,272,384]{2,1,0:T(8,128)(2,1)}), bf16[8,272,384]{2,1,0:T(8,128)(2,1)S(1)}, u32[]{:S(2)}, u32[]{:S(2)}) %all-to-all-start.1) | async-done | bytes 1671200 | tf_op jit(solution)/shard_map/all_to_all | solution.py:282
  184.3 0.3 convert_reduce_fusion.1
  184.7 0.1 fusion.1
  185.0 22.9 %all_to_all.20 = bf16[4,2,2,64,384]{4,3,1,2,0:T(8,128)(2,1)S(1)} all-to-all(bf16[4,2,2,64,384]{4,3,1,2,0:T(8,128)(2,1)S(1)} %pad_maximum_fusion), channel_id=1, replica_groups=mesh['win'=2,'bl'=4,'freq'=4] {'freq'}, dimensions={0} | all-to-all | bytes 1572864 | tf_op jit(solution)/shard_map/all_to_all | solution.py:288
  207.9 1.0 copy.28
  (34 shorter events, 0.8 us)
Async XLA Ops:
  7.3 34.6 %collective-permute-start = (bf16[16,384]{1,0:T(8,128)(2,1)S(1)}, bf16[16,384]{1,0:T(8,128)(2,1)S(1)}, u32[]{:S(2)}, u32[]{:S(2)}) collective-permute-start(bf16[16,384]{1,0:T(8,128)(2,1)S(1)} %get-tuple-element.18), channel_id=1, source_target_pairs={{0,3},{1,0},{2,1},{3,2},{4,7},{5,4},{6,5},{7,6},{8,11},{9,8},{10,9... | collective-permute-start | bytes 36872 | tf_op jit(solution)/shard_map/ppermute | solution.py:195
  12.3 29.5 %collective-permute-start.1 = (bf16[16,384]{1,0:T(8,128)(2,1)S(1)}, bf16[16,384]{1,0:T(8,128)(2,1)S(1)}, u32[]{:S(2)}, u32[]{:S(2)}) collective-permute-start(bf16[16,384]{1,0:T(8,128)(2,1)S(1)} %get-tuple-element.18), channel_id=1, source_target_pairs={{0,2},{1,3},{2,0},{3,1},{4,6},{5,7},{6,4},{7,5},{8,10},{9,11},{10,... | collective-permute-start | bytes 36872 | tf_op jit(solution)/shard_map/ppermute | solution.py:195
  12.3 29.6 %collective-permute-start.2 = (bf16[16,384]{1,0:T(8,128)(2,1)S(1)}, bf16[16,384]{1,0:T(8,128)(2,1)S(1)}, u32[]{:S(2)}, u32[]{:S(2)}) collective-permute-start(bf16[16,384]{1,0:T(8,128)(2,1)S(1)} %get-tuple-element.18), channel_id=1, source_target_pairs={{0,1},{1,2},{2,3},{3,0},{4,5},{5,6},{6,7},{7,4},{8,9},{9,10},{10,1... | collective-permute-start | bytes 36872 | tf_op jit(solution)/shard_map/ppermute | solution.py:195
  16.0 1.0 copy-start.4
  40.5 1.3 copy-start
  42.0 51.7 %all-to-all-start = ((bf16[4,16,2,64,128]{4,3,2,1,0:T(8,128)(2,1)}), bf16[4,16,2,64,128]{4,3,2,1,0:T(8,128)(2,1)S(1)}, u32[]{:S(2)}, u32[]{:S(2)}) async-start(bf16[4,16,2,64,128]{4,3,2,1,0:T(8,128)(2,1)} %copy-done), calls=%async_computation | async-start | bytes 4194304 | tf_op jit(solution)/shard_map/all_to_all | solution.py:243
  46.1 77.5 %all-gather.7.cloned.1.call-start = ((), (), s32[]{:S(2)}) async-start(), calls=%async_computation.5 | async-start | bytes 1310720 | tf_op jit(solution)/shard_map/all_gather | solution.py:278
  46.2 1.0 copy-start.5
  47.2 1.0 copy-start.6
  57.5 66.1 %copy-start.3 = (s32[16]{0:T(128)S(1)}, s32[16]{0:T(128)}, u32[]{:S(2)}) copy-start(s32[16]{0:T(128)} %ids_ref.3) | copy-start | bytes 196
  96.1 56.5 %all-gather.5.cloned.1.call-start = ((), (), s32[]{:S(2)}) async-start(), calls=%async_computation.4 | async-start | bytes 1310720 | tf_op jit(solution)/shard_map/all_gather | solution.py:278
  123.6 1.2 copy-start.2
  130.5 29.1 %all-to-all-start.2 = ((bf16[8,272,384]{2,1,0:T(8,128)(2,1)}), bf16[8,272,384]{2,1,0:T(8,128)(2,1)S(1)}, u32[]{:S(2)}, u32[]{:S(2)}) async-start(bf16[8,272,384]{2,1,0:T(8,128)(2,1)} %shard_map.77), calls=%async_computation.2 | async-start | bytes 3342336 | tf_op jit(solution)/shard_map/all_to_all | solution.py:282
  152.6 1.2 copy-start.1
  159.6 24.7 %all-to-all-start.1 = ((bf16[8,272,384]{2,1,0:T(8,128)(2,1)}), bf16[8,272,384]{2,1,0:T(8,128)(2,1)S(1)}, u32[]{:S(2)}, u32[]{:S(2)}) async-start(bf16[8,272,384]{2,1,0:T(8,128)(2,1)} %shard_map.76), calls=%async_computation.1 | async-start | bytes 3342336 | tf_op jit(solution)/shard_map/all_to_all | solution.py:282
Sparse Core Ops, SparseCore 0:
  96.3 27.2 all-gather.6
  125.2 27.4 all-gather.4

commit v3 on v2

--- a/solution.py
+++ b/solution.py
@@ -115,7 +115,97 @@
         inverse = halves(inverse_ref[i])
         for h, out_ref in enumerate(out_refs):
             total = jnp.sum(recv_ref[:, i, h].astype(jnp.float32), axis=0)
-            out_ref[i] = dot_split(halves(total), inverse).astype(jnp.bfloat16)
+            out_ref[0, i] = dot_split(halves(total), inverse).astype(jnp.bfloat16)
+
+
+def chain_kernel(shards, chunks, own_ref, out_ref, send_sem, recv_sem):
+    me = lax.axis_index("freq")
+    has_right, has_left = me < shards - 1, me > 0
+    barrier = pltpu.get_barrier_semaphore()
+
+    def greet(has, step):
+        @pl.when(has)
+        def _():
+            pl.semaphore_signal(
+                barrier, inc=1, device_id={"freq": me + step},
+                device_id_type=pl.DeviceIdType.MESH,
+            )
+
+    greet(has_right, 1)
+    greet(has_left, -1)
+    pl.semaphore_wait(barrier, has_right.astype(jnp.int32) + has_left.astype(jnp.int32))
+
+    def copy(way, h, hop, step):
+        source = me - step * hop
+        start = own_ref.at[h] if hop == 0 else out_ref.at[h, source]
+        return pltpu.make_async_remote_copy(
+            src_ref=start,
+            dst_ref=out_ref.at[h, source],
+            send_sem=send_sem.at[way, h, hop],
+            recv_sem=recv_sem.at[way, h, hop],
+            device_id={"freq": me + step},
+            device_id_type=pl.DeviceIdType.MESH,
+        )
+
+    def arrival(way, h, hop, step):
+        source = me - step * (hop + 1)
+        return pltpu.make_async_remote_copy(
+            src_ref=own_ref.at[h],
+            dst_ref=out_ref.at[h, source],
+            send_sem=send_sem.at[way, h, hop],
+            recv_sem=recv_sem.at[way, h, hop],
+            device_id={"freq": me - step},
+            device_id_type=pl.DeviceIdType.MESH,
+        )
+
+    ways = ((0, 1, has_right), (1, -1, has_left))
+    for hop in range(shards):
+        for h in range(chunks):
+            for way, step, has in ways:
+                source = me - step * hop
+                held = jnp.logical_and(source >= 0, source <= shards - 1)
+                if hop > 0:
+                    @pl.when(held)
+                    def _():
+                        arrival(way, h, hop - 1, step).wait_recv()
+                if hop < shards - 1:
+                    @pl.when(jnp.logical_and(held, has))
+                    def _():
+                        copy(way, h, hop, step).start()
+        if hop == 0:
+            for h in range(chunks):
+                out_ref[h, me] = own_ref[h]
+    for hop in range(shards - 1):
+        for h in range(chunks):
+            for way, step, has in ways:
+                source = me - step * hop
+                held = jnp.logical_and(source >= 0, source <= shards - 1)
+
+                @pl.when(jnp.logical_and(held, has))
+                def _():
+                    copy(way, h, hop, step).wait_send()
+
+
+def gather_chain(part, shards, chunks, call):
+    if shards > 8:
+        return jnp.stack([lax.all_gather(part[h], "freq") for h in range(chunks)])
+    hops = max(shards - 1, 1)
+    return pl.pallas_call(
+        functools.partial(chain_kernel, shards, chunks),
+        in_specs=[pl.BlockSpec(memory_space=pltpu.VMEM)],
+        out_specs=pl.BlockSpec(memory_space=pltpu.VMEM),
+        out_shape=jax.ShapeDtypeStruct((chunks, shards) + part.shape[1:], part.dtype),
+        scratch_shapes=[
+            pltpu.SemaphoreType.DMA((2, chunks, hops)),
+            pltpu.SemaphoreType.DMA((2, chunks, hops)),
+        ],
+        compiler_params=pltpu.CompilerParams(
+            collective_id=call, has_side_effects=True, vmem_limit_bytes=BIG
+        ),
+        cost_estimate=pl.CostEstimate(
+            flops=20_000_000_000, bytes_accessed=2 * shards * part.size, transcendentals=0
+        ),
+    )(part)
 
 
 def clean_kernel(ids_ref, fringe_ref, coef_ref, basis_t_ref, weight_ref, out_ref, total_ref):
@@ -127,7 +217,7 @@
 
     batch, size = fringe_ref.shape[0], fringe_ref.shape[1]
     for i in range(batch):
-        coef = coef_ref[:, i].astype(jnp.float32)
+        coef = coef_ref[0, :, i].astype(jnp.float32)
         coef = coef.reshape(-1, coef.shape[2]).astype(jnp.bfloat16)
         fitted = dot32(coef, basis_t_ref[...]) * weight_ref[i]
         group = ids_ref[item * batch + i]
@@ -247,8 +337,8 @@
         in_specs=[
             second((shards, batch, chunks, rows, DELAYS)), lead((batch, DELAYS, DELAYS)),
         ],
-        out_specs=[lead((batch, rows, DELAYS))] * chunks,
-        out_shape=[jax.ShapeDtypeStruct((items, rows, DELAYS), bf16)] * chunks,
+        out_specs=[second((1, batch, rows, DELAYS))] * chunks,
+        out_shape=[jax.ShapeDtypeStruct((1, items, rows, DELAYS), bf16)] * chunks,
         compiler_params=pltpu.CompilerParams(vmem_limit_bytes=BIG),
     )(received, inverse)
     basis_local_t = basis_local.T
@@ -262,7 +352,8 @@
                 grid=(items // batch,),
                 in_specs=[
                     pl.BlockSpec((batch, size, chan), lambda i, ids: (i, h, 0)),
-                    second((shards, batch, rows, DELAYS)), full((DELAYS, chan)),
+                    pl.BlockSpec((1, shards, batch, rows, DELAYS), lambda i, ids: (0, 0, i, 0, 0)),
+                    full((DELAYS, chan)),
                     lead((batch, 1, chan)),
                 ],
                 out_specs=full((groups, tall, chan)),
@@ -275,10 +366,12 @@
             ),
         )(group_id, fringe, gathered, basis_local_t, weight_rows)
 
-    gathered = [lax.all_gather(part, "freq") for part in coefficients]
     pieces = []
     for h in range(chunks):
-        sums = clean(h, gathered[h])
+        part = coefficients[h]
+        if h:
+            part, sums = lax.optimization_barrier((part, sums))
+        sums = clean(h, gather_chain(part, shards, 1, h))
         arrived = lax.all_to_all(sums, "bl", split_axis=0, concat_axis=0, tiled=True)
         total = jnp.sum(arrived.reshape(owners, GPO, tall, chan).astype(f32), 0)
         counts = jnp.maximum(total[:, size:size + 1, :1], 1.0)

time: 217 us -> 195 us (0.90)
  waiting for transfers between devices: 103 us -> 56.7 us
  Pallas kernels: 46.8 us -> 87 us
  between operations: 13.6 us -> 0.22 us
  local copies, waits for them, and re-layouts: 9.11 us -> 6.69 us
    all_gather x2 -> x0, waiting for transfers between devices: 45.2 us -> none  [per_device(): gathered = [lax.all_gather(part, 'freq') for part in coefficients]]
    pallas_call x0 -> x2, Pallas kernels: none -> 41.1 us  [gather_chain(): pl.pallas_call(functools.partial(chain_kernel, shards, chunks), in_specs=...]
    unnamed x20 -> x16, local copies, waits for them, and re-layouts: 6.87 us -> 4.44 us
  transfers between devices with their start and end apart: 8 -> 6, of which waited for: 4 -> 2; matrix products, arithmetic and copies ran while one was open for 1% -> 2% of each run, Pallas kernels for 21% -> 31%
where the time goes in v3:
time: 195 us; the launch traced here: 194 us
  Pallas kernels  87 us (45%)
  waiting for transfers between devices  56.7 us (29%)
  blocking collectives  22.6 us (12%)
  starting transfers between devices  17.7 us (9%)
  local copies, waits for them, and re-layouts  6.69 us (3%)
  other arithmetic  3.31 us (2%)
    pallas_call x2, Pallas kernels, gather_chain(): pl.pallas_call(functools.partial(chain_kernel, shards, chunks), in_specs=...  41.1 us
    all_to_all x1, waiting for transfers between devices, per_device(): lax.all_to_all(projected, 'freq', split_axis=0, concat_axis=0, tiled=True)  36.1 us
    pallas_call x1, Pallas kernels, per_device(): pl.pallas_call(functools.partial(filter_kernel, shards, chunks), grid=(it...  23.5 us
    all_to_all x1, blocking collectives, per_device(): lax.all_to_all(means, 'freq', split_axis=0, concat_axis=0, tiled=True)  22.6 us
    all_to_all x2, waiting for transfers between devices, per_device(): lax.all_to_all(sums, 'bl', split_axis=0, concat_axis=0, tiled=True)  20.6 us
    pallas_call x2, Pallas kernels, clean(): pl.pallas_call(clean_kernel, grid_spec=pltpu.PrefetchScalarGridSpec(num_s...  11.5 us
    pallas_call x1, Pallas kernels, per_device(): pl.pallas_call(functools.partial(inverse_kernel, batch, ridge, newton_sca...  9.37 us
    all_to_all x2, starting transfers between devices, per_device(): lax.all_to_all(sums, 'bl', split_axis=0, concat_axis=0, tiled=True)  7.14 us
  transfers between devices with their start and end apart: 6, of which 2 were waited for; matrix products, arithmetic and copies ran while one was open for 2% of the time, Pallas kernels for 31%

profile of v3, /device:TPU:0, one launch (start us, length us, event | category | flops | bytes accessed | tf_op | source)
XLA Modules:
  0.0 194.3 jit_solution(9568534349020077930)
XLA Ops:
  0.0 0.7 constant_dynamic-update-slice_fusion.7
  0.7 3.0 %collective-permute-start.2 = (bf16[16,384]{1,0:T(8,128)(2,1)S(1)}, bf16[16,384]{1,0:T(8,128)(2,1)S(1)}, u32[]{:S(2)}, u32[]{:S(2)}) collective-permute-start(bf16[16,384]{1,0:T(8,128)(2,1)S(1)} %get-tuple-element.20), channel_id=1, source_target_pairs={{0,1},{1,2},{2,3},{3,0},{4,5},{5,6},{6,7},{7,4},{8,9},{9,10},{10,1... | collective-permute-start | bytes 36872 | tf_op jit(solution)/shard_map/ppermute | solution.py:285
  3.8 2.6 %collective-permute-start.1 = (bf16[16,384]{1,0:T(8,128)(2,1)S(1)}, bf16[16,384]{1,0:T(8,128)(2,1)S(1)}, u32[]{:S(2)}, u32[]{:S(2)}) collective-permute-start(bf16[16,384]{1,0:T(8,128)(2,1)S(1)} %get-tuple-element.20), channel_id=1, source_target_pairs={{0,2},{1,3},{2,0},{3,1},{4,6},{5,7},{6,4},{7,5},{8,10},{9,11},{10,... | collective-permute-start | bytes 36872 | tf_op jit(solution)/shard_map/ppermute | solution.py:285
  6.4 1.3 collective-permute-start
  7.7 0.7 convert_subtract_fusion
  8.5 0.7 add_multiply_fusion.1
  9.3 0.9 dynamic-slice_bitcast_fusion.1
  10.2 0.1 copy.22.basis_ref
  10.3 1.0 copy-done.2
  11.4 23.5 %shard_map.73 = (bf16[16,512,384]{2,1,0:T(8,128)(2,1)}, bf16[4,16,2,64,128]{4,3,2,1,0:T(8,128)(2,1)S(1)}) custom-call(bf16[16,384,2,256]{3,2,1,0:T(2,128)(2,1)} %vis_ref.1, bf16[512,512]{1,0:T(8,128)(2,1)S(1)} %copy-done.2, bf16[512,512]{1,0:T(8,128)(2,1)S(1)} %copy-done.2, f32[16,1,512]{2,1,0:T(1,128)S(1)} %reshape.33.resp_ref, ...), custom_call_target="tpu_custom_call" | custom-call | flops 6442450944 | bytes 12582912 | tf_op jit(solution)/shard_map/pallas_call | solution.py:296
  34.9 1.4 copy-done
  36.4 3.6 %all-to-all-start = ((bf16[4,16,2,64,128]{4,3,2,1,0:T(8,128)(2,1)}), bf16[4,16,2,64,128]{4,3,2,1,0:T(8,128)(2,1)S(1)}, u32[]{:S(2)}, u32[]{:S(2)}) async-start(bf16[4,16,2,64,128]{4,3,2,1,0:T(8,128)(2,1)} %copy-done), calls=%async_computation | async-start | bytes 4194304 | tf_op jit(solution)/shard_map/all_to_all | solution.py:333
  40.1 1.0 copy-done.3
  41.1 1.0 copy-done.4
  42.1 9.4 %shard_map.74.inverse_ref = f32[16,128,128]{2,1,0:T(8,128)S(1)} custom-call(bf16[16,1,1536]{2,1,0:T(2,128)(2,1)S(1)} %copy.23.weight_ref, bf16[1536,128]{1,0:T(8,128)(2,1)S(1)} %copy-done.3, bf16[128,1536]{1,0:T(8,128)(2,1)S(1)} %copy-done.4), custom_call_target="tpu_custom_call" | custom-call | flops 20000000000 | bytes 1048576 | tf_op jit(solution)/shard_map/pallas_call | solution.py:319
  51.5 36.1 %all-to-all-done.recv_ref = bf16[4,16,2,64,128]{4,3,2,1,0:T(8,128)(2,1)S(1)} async-done(((bf16[4,16,2,64,128]{4,3,2,1,0:T(8,128)(2,1)}), bf16[4,16,2,64,128]{4,3,2,1,0:T(8,128)(2,1)S(1)}, u32[]{:S(2)}, u32[]{:S(2)}) %all-to-all-start) | async-done | bytes 2097184 | tf_op jit(solution)/shard_map/all_to_all | solution.py:333
  87.6 1.5 shard_map.75
  89.1 18.6 %shard_map.76.coef_ref = bf16[1,4,16,64,128]{4,3,2,1,0:T(8,128)(2,1)S(1)} custom-call(bf16[1,16,64,128]{3,2,1,0:T(8,128)(2,1)S(1)} %get-tuple-element.16.own_ref), custom_call_target="tpu_custom_call" | custom-call | flops 20000000000 | bytes 1048576 | tf_op jit(solution)/shard_map/pallas_call | solution.py:193
  107.7 5.8 %shard_map.77 = bf16[8,272,384]{2,1,0:T(8,128)(2,1)} custom-call(s32[16]{0:T(128)S(1)} %copy-done.1, bf16[16,512,384]{2,1,0:T(8,128)(2,1)} %get-tuple-element.12.fringe_ref, bf16[1,4,16,64,128]{4,3,2,1,0:T(8,128)(2,1)S(1)} %shard_map.76.coef_ref, bf16[128,384]{1,0:T(8,128)(2,1)S(1)} %get-tuple-element.21.basis_t_ref, f32[16,1,384]{2,1,0:T(1,128)S(1)} %reshape.34.weight_ref), custom_call_target="tpu_custom_call" | custom-call | flops 2000000000 | bytes 6291456 | tf_op jit(solution)/shard_map/pallas_call | solution.py:348
  113.5 3.6 %all-to-all-start.1 = ((bf16[8,272,384]{2,1,0:T(8,128)(2,1)}), bf16[8,272,384]{2,1,0:T(8,128)(2,1)S(1)}, u32[]{:S(2)}, u32[]{:S(2)}) async-start(bf16[8,272,384]{2,1,0:T(8,128)(2,1)} %shard_map.77), calls=%async_computation.1 | async-start | bytes 3342336 | tf_op jit(solution)/shard_map/all_to_all | solution.py:375
  117.1 22.5 %shard_map.78.coef_ref = bf16[1,4,16,64,128]{4,3,2,1,0:T(8,128)(2,1)S(1)} custom-call(bf16[1,16,64,128]{3,2,1,0:T(8,128)(2,1)S(1)} %get-tuple-element.18.own_ref), custom_call_target="tpu_custom_call" | custom-call | flops 20000000000 | bytes 1048576 | tf_op jit(solution)/shard_map/pallas_call | solution.py:193
  139.6 5.7 %shard_map.79 = bf16[8,272,384]{2,1,0:T(8,128)(2,1)} custom-call(s32[16]{0:T(128)S(1)} %copy-done.1, bf16[16,512,384]{2,1,0:T(8,128)(2,1)} %get-tuple-element.12.fringe_ref, bf16[1,4,16,64,128]{4,3,2,1,0:T(8,128)(2,1)S(1)} %shard_map.78.coef_ref, bf16[128,384]{1,0:T(8,128)(2,1)S(1)} %get-tuple-element.21.basis_t_ref, f32[16,1,384]{2,1,0:T(1,128)S(1)} %reshape.34.weight_ref), custom_call_target="tpu_custom_call" | custom-call | flops 2000000000 | bytes 6291456 | tf_op jit(solution)/shard_map/pallas_call | solution.py:348
  145.3 3.6 %all-to-all-start.2 = ((bf16[8,272,384]{2,1,0:T(8,128)(2,1)}), bf16[8,272,384]{2,1,0:T(8,128)(2,1)S(1)}, u32[]{:S(2)}, u32[]{:S(2)}) async-start(bf16[8,272,384]{2,1,0:T(8,128)(2,1)} %shard_map.79), calls=%async_computation.2 | async-start | bytes 3342336 | tf_op jit(solution)/shard_map/all_to_all | solution.py:375
  148.9 0.3 convert_reduce_fusion.1
  149.2 0.1 fusion.4
  149.3 0.1 fusion.1
  149.4 20.6 %all-to-all-done.2 = bf16[8,272,384]{2,1,0:T(8,128)(2,1)S(1)} async-done(((bf16[8,272,384]{2,1,0:T(8,128)(2,1)}), bf16[8,272,384]{2,1,0:T(8,128)(2,1)S(1)}, u32[]{:S(2)}, u32[]{:S(2)}) %all-to-all-start.2) | async-done | bytes 1671200 | tf_op jit(solution)/shard_map/all_to_all | solution.py:375
  170.0 0.3 convert_reduce_fusion
  170.3 0.1 fusion.5
  170.4 0.1 fusion
  170.7 22.6 %all_to_all.20 = bf16[4,2,2,64,384]{4,3,1,2,0:T(8,128)(2,1)S(1)} all-to-all(bf16[4,2,2,64,384]{4,3,1,2,0:T(8,128)(2,1)S(1)} %pad_maximum_fusion), channel_id=1, replica_groups=mesh['win'=2,'bl'=4,'freq'=4] {'freq'}, dimensions={0} | all-to-all | bytes 1572864 | tf_op jit(solution)/shard_map/all_to_all | solution.py:381
  193.3 1.0 copy.28
  (26 shorter events, 0.5 us)
Async XLA Ops:
  0.7 35.5 %collective-permute-start.2 = (bf16[16,384]{1,0:T(8,128)(2,1)S(1)}, bf16[16,384]{1,0:T(8,128)(2,1)S(1)}, u32[]{:S(2)}, u32[]{:S(2)}) collective-permute-start(bf16[16,384]{1,0:T(8,128)(2,1)S(1)} %get-tuple-element.20), channel_id=1, source_target_pairs={{0,1},{1,2},{2,3},{3,0},{4,5},{5,6},{6,7},{7,4},{8,9},{9,10},{10,1... | collective-permute-start | bytes 36872 | tf_op jit(solution)/shard_map/ppermute | solution.py:285
  3.8 32.5 %collective-permute-start.1 = (bf16[16,384]{1,0:T(8,128)(2,1)S(1)}, bf16[16,384]{1,0:T(8,128)(2,1)S(1)}, u32[]{:S(2)}, u32[]{:S(2)}) collective-permute-start(bf16[16,384]{1,0:T(8,128)(2,1)S(1)} %get-tuple-element.20), channel_id=1, source_target_pairs={{0,2},{1,3},{2,0},{3,1},{4,6},{5,7},{6,4},{7,5},{8,10},{9,11},{10,... | collective-permute-start | bytes 36872 | tf_op jit(solution)/shard_map/ppermute | solution.py:285
  6.4 29.9 %collective-permute-start = (bf16[16,384]{1,0:T(8,128)(2,1)S(1)}, bf16[16,384]{1,0:T(8,128)(2,1)S(1)}, u32[]{:S(2)}, u32[]{:S(2)}) collective-permute-start(bf16[16,384]{1,0:T(8,128)(2,1)S(1)} %get-tuple-element.20), channel_id=1, source_target_pairs={{0,3},{1,0},{2,1},{3,2},{4,7},{5,4},{6,5},{7,6},{8,11},{9,8},{10,9... | collective-permute-start | bytes 36872 | tf_op jit(solution)/shard_map/ppermute | solution.py:285
  10.3 1.0 copy-start.2
  34.9 1.4 copy-start
  36.4 51.2 %all-to-all-start = ((bf16[4,16,2,64,128]{4,3,2,1,0:T(8,128)(2,1)}), bf16[4,16,2,64,128]{4,3,2,1,0:T(8,128)(2,1)S(1)}, u32[]{:S(2)}, u32[]{:S(2)}) async-start(bf16[4,16,2,64,128]{4,3,2,1,0:T(8,128)(2,1)} %copy-done), calls=%async_computation | async-start | bytes 4194304 | tf_op jit(solution)/shard_map/all_to_all | solution.py:333
  40.1 1.0 copy-start.3
  41.1 1.0 copy-start.4
  89.1 18.7 %copy-start.1 = (s32[16]{0:T(128)S(1)}, s32[16]{0:T(128)}, u32[]{:S(2)}) copy-start(s32[16]{0:T(128)} %ids_ref.3) | copy-start | bytes 196
  113.5 31.8 %all-to-all-start.1 = ((bf16[8,272,384]{2,1,0:T(8,128)(2,1)}), bf16[8,272,384]{2,1,0:T(8,128)(2,1)S(1)}, u32[]{:S(2)}, u32[]{:S(2)}) async-start(bf16[8,272,384]{2,1,0:T(8,128)(2,1)} %shard_map.77), calls=%async_computation.1 | async-start | bytes 3342336 | tf_op jit(solution)/shard_map/all_to_all | solution.py:375
  145.3 24.7 %all-to-all-start.2 = ((bf16[8,272,384]{2,1,0:T(8,128)(2,1)}), bf16[8,272,384]{2,1,0:T(8,128)(2,1)S(1)}, u32[]{:S(2)}, u32[]{:S(2)}) async-start(bf16[8,272,384]{2,1,0:T(8,128)(2,1)} %shard_map.79), calls=%async_computation.2 | async-start | bytes 3342336 | tf_op jit(solution)/shard_map/all_to_all | solution.py:375

commit v4 on v3

--- a/solution.py
+++ b/solution.py
@@ -372,15 +372,34 @@
         if h:
             part, sums = lax.optimization_barrier((part, sums))
         sums = clean(h, gather_chain(part, shards, 1, h))
+        if h:
+            sums, pieces[-1] = lax.optimization_barrier((sums, pieces[-1]))
         arrived = lax.all_to_all(sums, "bl", split_axis=0, concat_axis=0, tiled=True)
         total = jnp.sum(arrived.reshape(owners, GPO, tall, chan).astype(f32), 0)
         counts = jnp.maximum(total[:, size:size + 1, :1], 1.0)
         mean = (total[:, :size] / counts).astype(bf16).reshape(GPO, shards, rows, chan)
         pieces.append(jnp.transpose(mean, (1, 0, 2, 3)))
-    means = jnp.stack(pieces, 1)
-    swapped = lax.all_to_all(means, "freq", split_axis=0, concat_axis=0, tiled=True)
-    averaged = jnp.transpose(swapped, (2, 1, 3, 0, 4))
-    return averaged.reshape(GPO, 2, time_local, CH)
+    if shards > 8:
+        swapped = [
+            lax.all_to_all(piece, "freq", split_axis=0, concat_axis=0, tiled=True)
+            for piece in pieces
+        ]
+        swapped = [jnp.concatenate(list(piece), axis=-1) for piece in swapped]
+    else:
+        me = lax.axis_index("freq")
+        swapped = []
+        for piece in pieces:
+            parts = [lax.dynamic_index_in_dim(piece, me, 0, keepdims=False)]
+            for j in range(1, shards):
+                out = lax.dynamic_index_in_dim(piece, (me + shards - j) % shards, 0, keepdims=False)
+                parts.append(
+                    lax.ppermute(out, "freq", [(d, (d - j) % shards) for d in range(shards)])
+                )
+            doubled = jnp.concatenate(parts + parts, axis=-1)
+            offset = (shards - me) % shards * chan
+            swapped.append(lax.dynamic_slice_in_dim(doubled, offset, CH, 2))
+    averaged = [piece.reshape(GPO, 2 // chunks, time_local, CH) for piece in swapped]
+    return jnp.concatenate(averaged, 1)
 
 
 def solution(mesh):

time: 195 us -> 184 us (0.944)
  blocking collectives: 22.6 us -> 0 us
  starting transfers between devices: 17.7 us -> 25.5 us
  waiting for transfers between devices: 56.7 us -> 59.7 us
    all_to_all x1 -> x0, blocking collectives: 22.6 us -> none  [per_device(): lax.all_to_all(means, 'freq', split_axis=0, concat_axis=0, tiled=True)]
    ppermute x0 -> x6, waiting for transfers between devices: none -> 13.5 us  [per_device(): lax.ppermute(out, 'freq', [(d, (d - j) % shards) for d in range(shards)])]
    all_to_all x2, waiting for transfers between devices: 20.6 us -> 10 us  [per_device(): lax.all_to_all(sums, 'bl', split_axis=0, concat_axis=0, tiled=True)]
    ppermute x0 -> x6, starting transfers between devices: none -> 7.74 us  [per_device(): lax.ppermute(out, 'freq', [(d, (d - j) % shards) for d in range(shards)])]
    unnamed x16 -> x30, local copies, waits for them, and re-layouts: 4.44 us -> 4.69 us
  transfers between devices with their start and end apart: 6 -> 12, of which waited for: 2 -> 6; matrix products, arithmetic and copies ran while one was open for 2% -> 2% of each run, Pallas kernels for 31% -> 33%
where the time goes in v4:
time: 184 us; the launch traced here: 183 us
  Pallas kernels  87.1 us (47%)
  waiting for transfers between devices  59.7 us (32%)
  starting transfers between devices  25.5 us (14%)
  local copies, waits for them, and re-layouts  6.07 us (3%)
  other arithmetic  4.17 us (2%)
    pallas_call x2, Pallas kernels, gather_chain(): pl.pallas_call(functools.partial(chain_kernel, shards, chunks), in_specs=...  41.1 us
    all_to_all x1, waiting for transfers between devices, per_device(): lax.all_to_all(projected, 'freq', split_axis=0, concat_axis=0, tiled=True)  36.1 us
    pallas_call x1, Pallas kernels, per_device(): pl.pallas_call(functools.partial(filter_kernel, shards, chunks), grid=(it...  23.5 us
    ppermute x6, waiting for transfers between devices, per_device(): lax.ppermute(out, 'freq', [(d, (d - j) % shards) for d in range(shards)])  13.5 us
    pallas_call x2, Pallas kernels, clean(): pl.pallas_call(clean_kernel, grid_spec=pltpu.PrefetchScalarGridSpec(num_s...  11.6 us
    all_to_all x2, waiting for transfers between devices, per_device(): lax.all_to_all(sums, 'bl', split_axis=0, concat_axis=0, tiled=True)  10 us
    pallas_call x1, Pallas kernels, per_device(): pl.pallas_call(functools.partial(inverse_kernel, batch, ridge, newton_sca...  9.37 us
    ppermute x6, starting transfers between devices, per_device(): lax.ppermute(out, 'freq', [(d, (d - j) % shards) for d in range(shards)])  7.74 us
  transfers between devices with their start and end apart: 12, of which 6 were waited for; matrix products, arithmetic and copies ran while one was open for 2% of the time, Pallas kernels for 33%

profile of v4, /device:TPU:0, one launch (start us, length us, event | category | flops | bytes accessed | tf_op | source)
XLA Modules:
  0.0 182.9 jit_solution(10997826186576668894)
XLA Ops:
  0.0 0.7 constant_dynamic-update-slice_fusion.7
  0.7 3.0 %collective-permute-start.2 = (bf16[16,384]{1,0:T(8,128)(2,1)S(1)}, bf16[16,384]{1,0:T(8,128)(2,1)S(1)}, u32[]{:S(2)}, u32[]{:S(2)}) collective-permute-start(bf16[16,384]{1,0:T(8,128)(2,1)S(1)} %get-tuple-element.24), channel_id=1, source_target_pairs={{0,1},{1,2},{2,3},{3,0},{4,5},{5,6},{6,7},{7,4},{8,9},{9,10},{10,1... | collective-permute-start | bytes 36872 | tf_op jit(solution)/shard_map/ppermute | solution.py:285
  3.8 2.6 %collective-permute-start.1 = (bf16[16,384]{1,0:T(8,128)(2,1)S(1)}, bf16[16,384]{1,0:T(8,128)(2,1)S(1)}, u32[]{:S(2)}, u32[]{:S(2)}) collective-permute-start(bf16[16,384]{1,0:T(8,128)(2,1)S(1)} %get-tuple-element.24), channel_id=1, source_target_pairs={{0,2},{1,3},{2,0},{3,1},{4,6},{5,7},{6,4},{7,5},{8,10},{9,11},{10,... | collective-permute-start | bytes 36872 | tf_op jit(solution)/shard_map/ppermute | solution.py:285
  6.4 1.3 collective-permute-start
  7.7 0.7 convert_subtract_fusion
  8.5 0.7 add_multiply_fusion.1
  9.3 0.9 dynamic-slice_bitcast_fusion.9
  10.3 1.0 copy-done.2
  11.4 23.5 %shard_map.73 = (bf16[16,512,384]{2,1,0:T(8,128)(2,1)}, bf16[4,16,2,64,128]{4,3,2,1,0:T(8,128)(2,1)S(1)}) custom-call(bf16[16,384,2,256]{3,2,1,0:T(2,128)(2,1)} %vis_ref.1, bf16[512,512]{1,0:T(8,128)(2,1)S(1)} %copy-done.2, bf16[512,512]{1,0:T(8,128)(2,1)S(1)} %copy-done.2, f32[16,1,512]{2,1,0:T(1,128)S(1)} %reshape.44.resp_ref, ...), custom_call_target="tpu_custom_call" | custom-call | flops 6442450944 | bytes 12582912 | tf_op jit(solution)/shard_map/pallas_call | solution.py:296
  34.9 1.3 copy-done
  36.4 3.6 %all-to-all-start = ((bf16[4,16,2,64,128]{4,3,2,1,0:T(8,128)(2,1)}), bf16[4,16,2,64,128]{4,3,2,1,0:T(8,128)(2,1)S(1)}, u32[]{:S(2)}, u32[]{:S(2)}) async-start(bf16[4,16,2,64,128]{4,3,2,1,0:T(8,128)(2,1)} %copy-done), calls=%async_computation | async-start | bytes 4194304 | tf_op jit(solution)/shard_map/all_to_all | solution.py:333
  40.1 1.0 copy-done.3
  41.1 1.0 copy-done.4
  42.1 9.4 %shard_map.74.inverse_ref = f32[16,128,128]{2,1,0:T(8,128)S(1)} custom-call(bf16[16,1,1536]{2,1,0:T(2,128)(2,1)S(1)} %copy.33.weight_ref, bf16[1536,128]{1,0:T(8,128)(2,1)S(1)} %copy-done.3, bf16[128,1536]{1,0:T(8,128)(2,1)S(1)} %copy-done.4), custom_call_target="tpu_custom_call" | custom-call | flops 20000000000 | bytes 1048576 | tf_op jit(solution)/shard_map/pallas_call | solution.py:319
  51.5 36.1 %all-to-all-done.recv_ref = bf16[4,16,2,64,128]{4,3,2,1,0:T(8,128)(2,1)S(1)} async-done(((bf16[4,16,2,64,128]{4,3,2,1,0:T(8,128)(2,1)}), bf16[4,16,2,64,128]{4,3,2,1,0:T(8,128)(2,1)S(1)}, u32[]{:S(2)}, u32[]{:S(2)}) %all-to-all-start) | async-done | bytes 2097184 | tf_op jit(solution)/shard_map/all_to_all | solution.py:333
  87.6 1.5 shard_map.75
  89.1 18.6 %shard_map.76.coef_ref = bf16[1,4,16,64,128]{4,3,2,1,0:T(8,128)(2,1)S(1)} custom-call(bf16[1,16,64,128]{3,2,1,0:T(8,128)(2,1)S(1)} %get-tuple-element.19.own_ref), custom_call_target="tpu_custom_call" | custom-call | flops 20000000000 | bytes 1048576 | tf_op jit(solution)/shard_map/pallas_call | solution.py:193
  107.7 5.8 %shard_map.77 = bf16[8,272,384]{2,1,0:T(8,128)(2,1)} custom-call(s32[16]{0:T(128)S(1)} %copy-done.1, bf16[16,512,384]{2,1,0:T(8,128)(2,1)} %get-tuple-element.14.fringe_ref, bf16[1,4,16,64,128]{4,3,2,1,0:T(8,128)(2,1)S(1)} %shard_map.76.coef_ref, bf16[128,384]{1,0:T(8,128)(2,1)S(1)} %get-tuple-element.31.basis_t_ref, f32[16,1,384]{2,1,0:T(1,128)S(1)} %reshape.45.weight_ref), custom_call_target="tpu_custom_call" | custom-call | flops 2000000000 | bytes 6291456 | tf_op jit(solution)/shard_map/pallas_call | solution.py:348
  113.6 3.6 %all-to-all-start.1 = ((bf16[8,272,384]{2,1,0:T(8,128)(2,1)}), bf16[8,272,384]{2,1,0:T(8,128)(2,1)S(1)}, u32[]{:S(2)}, u32[]{:S(2)}) async-start(bf16[8,272,384]{2,1,0:T(8,128)(2,1)} %shard_map.77), calls=%async_computation.1 | async-start | bytes 3342336 | tf_op jit(solution)/shard_map/all_to_all | solution.py:377
  117.2 22.5 %shard_map.78.coef_ref = bf16[1,4,16,64,128]{4,3,2,1,0:T(8,128)(2,1)S(1)} custom-call(bf16[1,16,64,128]{3,2,1,0:T(8,128)(2,1)S(1)} %get-tuple-element.20.own_ref), custom_call_target="tpu_custom_call" | custom-call | flops 20000000000 | bytes 1048576 | tf_op jit(solution)/shard_map/pallas_call | solution.py:193
  139.7 5.7 %shard_map.79 = bf16[8,272,384]{2,1,0:T(8,128)(2,1)} custom-call(s32[16]{0:T(128)S(1)} %copy-done.1, bf16[16,512,384]{2,1,0:T(8,128)(2,1)} %get-tuple-element.14.fringe_ref, bf16[1,4,16,64,128]{4,3,2,1,0:T(8,128)(2,1)S(1)} %shard_map.78.coef_ref, bf16[128,384]{1,0:T(8,128)(2,1)S(1)} %get-tuple-element.31.basis_t_ref, f32[16,1,384]{2,1,0:T(1,128)S(1)} %reshape.45.weight_ref), custom_call_target="tpu_custom_call" | custom-call | flops 2000000000 | bytes 6291456 | tf_op jit(solution)/shard_map/pallas_call | solution.py:348
  145.9 3.6 %all-to-all-start.2 = ((bf16[8,272,384]{2,1,0:T(8,128)(2,1)}), bf16[8,272,384]{2,1,0:T(8,128)(2,1)S(1)}, u32[]{:S(2)}, u32[]{:S(2)}) async-start(bf16[8,272,384]{2,1,0:T(8,128)(2,1)} %shard_map.79), calls=%async_computation.2 | async-start | bytes 3342336 | tf_op jit(solution)/shard_map/all_to_all | solution.py:377
  149.6 2.1 %collective-permute-start.4 = (bf16[2,64,384]{2,1,0:T(8,128)(2,1)S(1)}, bf16[2,64,384]{2,1,0:T(8,128)(2,1)S(1)}, u32[]{:S(2)}, u32[]{:S(2)}) collective-permute-start(bf16[2,64,384]{2,1,0:T(8,128)(2,1)S(1)} %get-tuple-element.26), channel_id=1, source_target_pairs={{0,2},{1,3},{2,0},{3,1},{4,6},{5,7},{6,4},{7,5},{8,10},{9,11},{10,... | collective-permute-start | bytes 294920 | tf_op jit(solution)/shard_map/ppermute | solution.py:396
  151.7 1.7 collective-permute-start.3
  153.4 5.7 %collective-permute-done.3 = bf16[2,64,384]{2,1,0:T(8,128)(2,1)S(1)} collective-permute-done((bf16[2,64,384]{2,1,0:T(8,128)(2,1)S(1)}, bf16[2,64,384]{2,1,0:T(8,128)(2,1)S(1)}, u32[]{:S(2)}, u32[]{:S(2)}) %collective-permute-start.3) | collective-permute-done | bytes 98336 | tf_op jit(solution)/shard_map/ppermute | solution.py:396
  159.2 1.2 collective-permute-done.4
  160.6 10.0 %all-to-all-done.2 = bf16[8,272,384]{2,1,0:T(8,128)(2,1)S(1)} async-done(((bf16[8,272,384]{2,1,0:T(8,128)(2,1)}), bf16[8,272,384]{2,1,0:T(8,128)(2,1)S(1)}, u32[]{:S(2)}, u32[]{:S(2)}) %all-to-all-start.2) | async-done | bytes 1671200 | tf_op jit(solution)/shard_map/all_to_all | solution.py:377
  171.2 2.1 %collective-permute-start.7 = (bf16[2,64,384]{2,1,0:T(8,128)(2,1)S(1)}, bf16[2,64,384]{2,1,0:T(8,128)(2,1)S(1)}, u32[]{:S(2)}, u32[]{:S(2)}) collective-permute-start(bf16[2,64,384]{2,1,0:T(8,128)(2,1)S(1)} %get-tuple-element.29), channel_id=1, source_target_pairs={{0,2},{1,3},{2,0},{3,1},{4,6},{5,7},{6,4},{7,5},{8,10},{9,11},{10,... | collective-permute-start | bytes 294920 | tf_op jit(solution)/shard_map/ppermute | solution.py:396
  173.3 1.7 collective-permute-start.6
  175.0 5.1 %collective-permute-done.6 = bf16[2,64,384]{2,1,0:T(8,128)(2,1)S(1)} collective-permute-done((bf16[2,64,384]{2,1,0:T(8,128)(2,1)S(1)}, bf16[2,64,384]{2,1,0:T(8,128)(2,1)S(1)}, u32[]{:S(2)}, u32[]{:S(2)}) %collective-permute-start.6) | collective-permute-done | bytes 98336 | tf_op jit(solution)/shard_map/ppermute | solution.py:396
  180.1 1.6 collective-permute-done.7
  181.9 1.0 pad_maximum_fusion
  (55 shorter events, 2.0 us)
Async XLA Ops:
  0.7 35.5 %collective-permute-start.2 = (bf16[16,384]{1,0:T(8,128)(2,1)S(1)}, bf16[16,384]{1,0:T(8,128)(2,1)S(1)}, u32[]{:S(2)}, u32[]{:S(2)}) collective-permute-start(bf16[16,384]{1,0:T(8,128)(2,1)S(1)} %get-tuple-element.24), channel_id=1, source_target_pairs={{0,1},{1,2},{2,3},{3,0},{4,5},{5,6},{6,7},{7,4},{8,9},{9,10},{10,1... | collective-permute-start | bytes 36872 | tf_op jit(solution)/shard_map/ppermute | solution.py:285
  3.8 32.5 %collective-permute-start.1 = (bf16[16,384]{1,0:T(8,128)(2,1)S(1)}, bf16[16,384]{1,0:T(8,128)(2,1)S(1)}, u32[]{:S(2)}, u32[]{:S(2)}) collective-permute-start(bf16[16,384]{1,0:T(8,128)(2,1)S(1)} %get-tuple-element.24), channel_id=1, source_target_pairs={{0,2},{1,3},{2,0},{3,1},{4,6},{5,7},{6,4},{7,5},{8,10},{9,11},{10,... | collective-permute-start | bytes 36872 | tf_op jit(solution)/shard_map/ppermute | solution.py:285
  6.4 29.9 %collective-permute-start = (bf16[16,384]{1,0:T(8,128)(2,1)S(1)}, bf16[16,384]{1,0:T(8,128)(2,1)S(1)}, u32[]{:S(2)}, u32[]{:S(2)}) collective-permute-start(bf16[16,384]{1,0:T(8,128)(2,1)S(1)} %get-tuple-element.24), channel_id=1, source_target_pairs={{0,3},{1,0},{2,1},{3,2},{4,7},{5,4},{6,5},{7,6},{8,11},{9,8},{10,9... | collective-permute-start | bytes 36872 | tf_op jit(solution)/shard_map/ppermute | solution.py:285
  10.3 1.0 copy-start.2
  34.9 1.3 copy-start
  36.4 51.2 %all-to-all-start = ((bf16[4,16,2,64,128]{4,3,2,1,0:T(8,128)(2,1)}), bf16[4,16,2,64,128]{4,3,2,1,0:T(8,128)(2,1)S(1)}, u32[]{:S(2)}, u32[]{:S(2)}) async-start(bf16[4,16,2,64,128]{4,3,2,1,0:T(8,128)(2,1)} %copy-done), calls=%async_computation | async-start | bytes 4194304 | tf_op jit(solution)/shard_map/all_to_all | solution.py:333
  40.1 1.0 copy-start.3
  41.1 1.0 copy-start.4
  89.1 18.7 %copy-start.1 = (s32[16]{0:T(128)S(1)}, s32[16]{0:T(128)}, u32[]{:S(2)}) copy-start(s32[16]{0:T(128)} %ids_ref.3) | copy-start | bytes 196
  113.6 31.8 %all-to-all-start.1 = ((bf16[8,272,384]{2,1,0:T(8,128)(2,1)}), bf16[8,272,384]{2,1,0:T(8,128)(2,1)S(1)}, u32[]{:S(2)}, u32[]{:S(2)}) async-start(bf16[8,272,384]{2,1,0:T(8,128)(2,1)} %shard_map.77), calls=%async_computation.1 | async-start | bytes 3342336 | tf_op jit(solution)/shard_map/all_to_all | solution.py:377
  145.9 24.7 %all-to-all-start.2 = ((bf16[8,272,384]{2,1,0:T(8,128)(2,1)}), bf16[8,272,384]{2,1,0:T(8,128)(2,1)S(1)}, u32[]{:S(2)}, u32[]{:S(2)}) async-start(bf16[8,272,384]{2,1,0:T(8,128)(2,1)} %shard_map.79), calls=%async_computation.2 | async-start | bytes 3342336 | tf_op jit(solution)/shard_map/all_to_all | solution.py:377
  149.6 10.9 %collective-permute-start.5 = (bf16[2,64,384]{2,1,0:T(8,128)(2,1)S(1)}, bf16[2,64,384]{2,1,0:T(8,128)(2,1)S(1)}, u32[]{:S(2)}, u32[]{:S(2)}) collective-permute-start(bf16[2,64,384]{2,1,0:T(8,128)(2,1)S(1)} %get-tuple-element.25), channel_id=1, source_target_pairs={{0,1},{1,2},{2,3},{3,0},{4,5},{5,6},{6,7},{7,4},{8,9},{9,10},{10,1... | collective-permute-start | bytes 294920 | tf_op jit(solution)/shard_map/ppermute | solution.py:396
  149.6 10.8 %collective-permute-start.4 = (bf16[2,64,384]{2,1,0:T(8,128)(2,1)S(1)}, bf16[2,64,384]{2,1,0:T(8,128)(2,1)S(1)}, u32[]{:S(2)}, u32[]{:S(2)}) collective-permute-start(bf16[2,64,384]{2,1,0:T(8,128)(2,1)S(1)} %get-tuple-element.26), channel_id=1, source_target_pairs={{0,2},{1,3},{2,0},{3,1},{4,6},{5,7},{6,4},{7,5},{8,10},{9,11},{10,... | collective-permute-start | bytes 294920 | tf_op jit(solution)/shard_map/ppermute | solution.py:396
  151.7 7.5 %collective-permute-start.3 = (bf16[2,64,384]{2,1,0:T(8,128)(2,1)S(1)}, bf16[2,64,384]{2,1,0:T(8,128)(2,1)S(1)}, u32[]{:S(2)}, u32[]{:S(2)}) collective-permute-start(bf16[2,64,384]{2,1,0:T(8,128)(2,1)S(1)} %get-tuple-element.27), channel_id=1, source_target_pairs={{0,3},{1,0},{2,1},{3,2},{4,7},{5,4},{6,5},{7,6},{8,11},{9,8},{10,9... | collective-permute-start | bytes 294920 | tf_op jit(solution)/shard_map/ppermute | solution.py:396
  171.2 10.6 %collective-permute-start.8 = (bf16[2,64,384]{2,1,0:T(8,128)(2,1)S(1)}, bf16[2,64,384]{2,1,0:T(8,128)(2,1)S(1)}, u32[]{:S(2)}, u32[]{:S(2)}) collective-permute-start(bf16[2,64,384]{2,1,0:T(8,128)(2,1)S(1)} %get-tuple-element.28), channel_id=1, source_target_pairs={{0,1},{1,2},{2,3},{3,0},{4,5},{5,6},{6,7},{7,4},{8,9},{9,10},{10,1... | collective-permute-start | bytes 294920 | tf_op jit(solution)/shard_map/ppermute | solution.py:396
  171.2 10.5 %collective-permute-start.7 = (bf16[2,64,384]{2,1,0:T(8,128)(2,1)S(1)}, bf16[2,64,384]{2,1,0:T(8,128)(2,1)S(1)}, u32[]{:S(2)}, u32[]{:S(2)}) collective-permute-start(bf16[2,64,384]{2,1,0:T(8,128)(2,1)S(1)} %get-tuple-element.29), channel_id=1, source_target_pairs={{0,2},{1,3},{2,0},{3,1},{4,6},{5,7},{6,4},{7,5},{8,10},{9,11},{10,... | collective-permute-start | bytes 294920 | tf_op jit(solution)/shard_map/ppermute | solution.py:396
  173.3 6.8 %collective-permute-start.6 = (bf16[2,64,384]{2,1,0:T(8,128)(2,1)S(1)}, bf16[2,64,384]{2,1,0:T(8,128)(2,1)S(1)}, u32[]{:S(2)}, u32[]{:S(2)}) collective-permute-start(bf16[2,64,384]{2,1,0:T(8,128)(2,1)S(1)} %get-tuple-element.30), channel_id=1, source_target_pairs={{0,3},{1,0},{2,1},{3,2},{4,7},{5,4},{6,5},{7,6},{8,11},{9,8},{10,9... | collective-permute-start | bytes 294920 | tf_op jit(solution)/shard_map/ppermute | solution.py:396
